TPU v7x, 32 devices: a whole 2x2x4 slice. The times are simulated.
32 devices in a mesh: grp: 2 (over x), seq: 16 (over z, y, core).
Axes of the slice: x: 2, y: 2, z: 4, core: 2. Of those that a mesh axis runs over, the one named last changes fastest.
Arguments:
- hidden: bfloat16 [4, 5120, 1280], P('grp', 'seq'), parts along dimension 0, may hold values from -160 to 160
- mod_shift: float32 [5120], replicated, may hold values from -3 to 3
- mod_scale: float32 [5120], replicated, may hold values from -0.5 to 0.5
- head_weight: float32 [64, 5120], replicated, may hold values from -0.078125 to 0.078125
- head_bias: float32 [64], replicated, may hold values from -3 to 3
- conv_in_weight: bfloat16 [3, 3, 3, 16, 384], replicated, may hold values from -0.3125 to 0.3125
- conv_in_bias: float32 [384], replicated, may hold values from -3 to 3
- gain_in: float32 [384], replicated, may hold values from 0.1 to 1.9
- up_weight: bfloat16 [3, 3, 384, 192], replicated, may hold values from -0.109375 to 0.109375
- up_bias: float32 [192], replicated, may hold values from -3 to 3
- gain_up: float32 [192], replicated, may hold values from 0.1 to 1.9
- out_weight: bfloat16 [3, 3, 3, 192, 96], replicated, may hold values from -0.078125 to 0.078125
- out_bias: float32 [96], replicated, may hold values from -2 to 2
Outputs:
- decoded: bfloat16 [4, 64, 320, 96], P('grp', 'seq'), parts along dimension 0
There are 2 independent parts, one for each index of `grp`. A program takes and returns all parts, laid end to end along the dimension named above; an argument that names none is the same for every part. Nothing has to cross between parts.
All inputs are finite; a program needn't handle non-finite values.
Results may differ from a plain program's by a relative error of at most 0.0056.
Values may be sent and summed in bfloat16 or wider, within the bound.
A program may use at most 64 MiB of HBM per device.

v0:
```python
import functools

import jax
import jax.numpy as jnp
from jax import lax
from jax.experimental import pallas as pl
from jax.experimental.pallas import tpu as pltpu
from jax.sharding import PartitionSpec as P

TOK_W = 80
HIGH = lax.Precision.HIGHEST
F32 = jnp.float32
BF16 = jnp.bfloat16


def rms_silu(values, gain_vec):
    squares = jnp.mean(values * values, axis=-1, keepdims=True)
    normed = values * lax.rsqrt(squares + 1e-06) * gain_vec
    return normed * jax.nn.sigmoid(normed)


def shift_cols(values, step):
    count = values.shape[0]
    col = lax.broadcasted_iota(jnp.int32, (count, 1), 0) % TOK_W
    if step > 0:
        return jnp.where(col == 0, 0.0, pltpu.roll(values, 1, 0))
    return jnp.where(col == TOK_W - 1, 0.0, pltpu.roll(values, count - 1, 0))


def conv_kernel(num_dev, lat_rows, chans, pos_ref, x_ref, w1_ref, b1_ref, g1_ref, w2_ref, b2_ref, g2_ref,
                w3_ref, b3_ref, out_ref, act1, act2, res, w1s):
    c1, c2, c3 = chans
    ch = w1_ref.shape[3]
    blank = jnp.zeros((ch, c1), BF16)
    for a in range(2):
        for b in range(3):
            for j in range(4):
                rows = slice((4 * b + j) * ch, (4 * b + j + 1) * ch)
                w1s[a, rows, 0:c1] = w1_ref[a + 1, b, j] if j < 3 else blank
                w1s[a, rows, c1 : 2 * c1] = w1_ref[a + 1, b, j - 1] if j > 0 else blank
    dev = pos_ref[0]
    rows1 = lat_rows + 2
    m1 = rows1 * TOK_W
    rows2 = lat_rows + 1
    m2 = rows2 * TOK_W
    rows3 = 2 * lat_rows
    m3 = rows3 * TOK_W

    def inside(count, first, step, total):
        row = lax.broadcasted_iota(jnp.int32, (count, 1), 0) // TOK_W * step + first
        return (row >= 0) & (row < total)

    keep1 = inside(m1, dev * lat_rows - 1, 1, num_dev * lat_rows)
    for frame in range(2):
        x_now = x_ref[frame].reshape(m1, x_ref.shape[-1])
        pre = jnp.dot(x_now, w1s[1], preferred_element_type=F32)
        if frame == 1:
            x_old = x_ref[0].reshape(m1, x_ref.shape[-1])
            pre = pre + jnp.dot(x_old, w1s[0], preferred_element_type=F32)
        for r in range(2):
            val = rms_silu(pre[:, r * c1 : (r + 1) * c1] + b1_ref[...], g1_ref[...])
            val = jnp.where(keep1, val, 0.0)
            edge = shift_cols(val, 1) if r == 1 else shift_cols(val, -1)
            spot = 0 if r == 1 else 3
            act1[frame, :, :, (r + 1) * c1 : (r + 2) * c1] = val.astype(BF16).reshape(rows1, TOK_W, c1)
            act1[frame, :, :, spot * c1 : (spot + 1) * c1] = edge.astype(BF16).reshape(rows1, TOK_W, c1)

    start = (0, 1, 1, 2)
    for p in range(2):
        first = 0 if p == 0 else -1
        keep2 = inside(m2, 2 * dev * lat_rows + first, 2, 2 * num_dev * lat_rows)
        for frame in range(2):
            for s in range(4):
                q = s % 2
                lanes = slice(start[s] * c1, (start[s] + 2) * c1)
                top = act1[frame, 0:rows2, :, lanes].reshape(m2, 2 * c1)
                low = act1[frame, 1 : rows2 + 1, :, lanes].reshape(m2, 2 * c1)
                pre = jnp.dot(top, w2_ref[p, 0, q], preferred_element_type=F32)
                pre = pre + jnp.dot(low, w2_ref[p, 1, q], preferred_element_type=F32)
                val = rms_silu(pre + b2_ref[...], g2_ref[...])
                val = jnp.where(keep2, val, 0.0)
                val = jnp.concatenate([val, jnp.zeros((m2, 256 - c2), F32)], axis=1)
                pieces = [(s + 1, val)]
                if s == 3:
                    pieces.append((0, shift_cols(val, 1)))
                if s == 0:
                    pieces.append((5, shift_cols(val, -1)))
                for spot, piece in pieces:
                    piece = piece.astype(BF16).reshape(rows2, TOK_W, 256)
                    for i in range(rows2):
                        act2[frame, 2 * i + 1 - p, :, spot * 256 : (spot + 1) * 256] = piece[i]

    for s in range(4):
        lanes = slice(s * 256, (s + 3) * 256)
        old = None
        new = None
        for b in range(3):
            before = act2[0, b : b + rows3, :, lanes].reshape(m3, 768)
            after = act2[1, b : b + rows3, :, lanes].reshape(m3, 768)
            one = jnp.dot(before, w3_ref[b], preferred_element_type=F32)
            two = jnp.dot(after, w3_ref[b, :, 0:128], preferred_element_type=F32)
            old = one if old is None else old + one
            new = two if new is None else new + two
        res[pl.ds(s, m3, stride=4), :] = old[:, 0:128] + b3_ref[...]
        res[pl.ds(4 * m3 + s, m3, stride=4), :] = old[:, 128:256] + new + b3_ref[...]
    width = 4 * TOK_W
    for i in range(2 * rows3):
        out_ref[i] = jnp.transpose(res[i * width : (i + 1) * width, :])[0:c3].astype(BF16)


def decode(x1, dev_index, num_dev, conv_in_weight, conv_in_bias, gain_in, up_weight, up_bias, gain_up, out_weight, out_bias):
    frames, rows1, cols, _ = x1.shape
    lat_rows = rows1 - 2
    lat_ch, c1 = conv_in_weight.shape[3:]
    c2, c3 = out_weight.shape[3:]
    wide = up_weight.astype(F32)
    by_row = jnp.stack(
        [jnp.stack([wide[0], wide[1] + wide[2]]), jnp.stack([wide[0] + wide[1], wide[2]])]
    )
    by_col = jnp.stack(
        [
            jnp.stack([by_row[:, :, 0], by_row[:, :, 1] + by_row[:, :, 2]], axis=2),
            jnp.stack([by_row[:, :, 0] + by_row[:, :, 1], by_row[:, :, 2]], axis=2),
        ],
        axis=2,
    )
    w2 = by_col.astype(BF16).reshape(2, 2, 2, 2 * c1, c2)
    w3 = jnp.pad(out_weight[1:], ((0, 0), (0, 0), (0, 0), (0, 256 - c2), (0, 128 - c3)))
    w3 = jnp.concatenate([w3[1], w3[0]], axis=-1).reshape(3, 768, 256)
    b3 = jnp.pad(out_bias, (0, 128 - c3))[None]
    cells = frames * 2 * lat_rows * 4 * cols
    vmem = pl.BlockSpec(memory_space=pltpu.VMEM)
    out = pl.pallas_call(
        functools.partial(conv_kernel, num_dev, lat_rows, (c1, c2, c3)),
        out_shape=jax.ShapeDtypeStruct((frames * 2 * lat_rows, c3, 4 * cols), BF16),
        in_specs=[pl.BlockSpec(memory_space=pltpu.SMEM)] + [vmem] * 9,
        out_specs=vmem,
        scratch_shapes=[
            pltpu.VMEM((frames, rows1, cols, 4 * c1), BF16),
            pltpu.VMEM((frames, 2 * lat_rows + 2, cols, 6 * 256), BF16),
            pltpu.VMEM((cells, 128), F32),
            pltpu.VMEM((2, 12 * lat_ch, 2 * c1), BF16),
        ],
        compiler_params=pltpu.CompilerParams(vmem_limit_bytes=40 * 1024 * 1024),
    )(dev_index[None].astype(jnp.int32), x1, conv_in_weight, conv_in_bias[None], gain_in[None], w2, up_bias[None], gain_up[None], w3, b3)
    return out.reshape(frames, 2 * lat_rows, c3, 4 * cols).transpose(0, 1, 3, 2)


def head_kernel(num_dev, x_ref, w_ref, out_ref):
    frames, feat, total = x_ref.shape
    tile = total // num_dev
    weight = w_ref[...]
    patch = weight.shape[0]
    high = weight.astype(BF16)
    rest = weight - high.astype(F32)
    mid = rest.astype(BF16)
    low = (rest - mid.astype(F32)).astype(BF16)
    stack = jnp.concatenate([high, mid, low], axis=0)
    sums = jnp.sum(weight, axis=1, keepdims=True)
    parts, means, spreads = [], [], []
    for f in range(frames):
        full = jnp.dot(stack, x_ref[f], preferred_element_type=F32)
        values = x_ref[f].astype(F32)
        mean = jnp.sum(values, axis=0, keepdims=True) * (1.0 / feat)
        centred = values - mean
        means.append(mean)
        spreads.append(jnp.sum(centred * centred, axis=0, keepdims=True))
        part = full[:patch] + (full[patch : 2 * patch] + full[2 * patch :])
        parts.append(part - sums * mean)
    both = jnp.concatenate(parts, axis=0)
    out_ref[:, 0:tile, :] = jnp.transpose(both).reshape(num_dev, tile, frames * patch)
    out_ref[:, tile : tile + 8, :] = jnp.zeros((num_dev, 8, frames * patch), F32)
    stats = jnp.concatenate(means + spreads, axis=0)
    for i in range(num_dev):
        out_ref[i, tile : tile + 2 * frames, 0:tile] = stats[:, i * tile : (i + 1) * tile]


def merge_kernel(feat, tile, got_ref, sums_ref, base_ref, out_ref):
    num_dev = got_ref.shape[0]
    patch = sums_ref.shape[1]
    for f in range(2):
        means = got_ref[:, tile + f, :]
        off = means - jnp.mean(means, axis=0, keepdims=True)
        spread = jnp.sum(got_ref[:, tile + 2 + f, :], axis=0, keepdims=True)
        var = (spread + feat * jnp.sum(off * off, axis=0, keepdims=True)) * (1.0 / (feat * num_dev))
        scale = jnp.transpose(jnp.broadcast_to(lax.rsqrt(var + 1e-06), (8, var.shape[1])))[0:tile, 0:1]
        fixed = jnp.dot(jnp.transpose(off), sums_ref[...], precision=HIGH, preferred_element_type=F32)
        summed = jnp.sum(got_ref[:, 0:tile, :], axis=0)[:, f * patch : (f + 1) * patch] + fixed[0:tile]
        out_ref[f] = (summed * scale + base_ref[...]).astype(BF16)


def local(
    hidden, mod_shift, mod_scale, head_weight, head_bias, conv_in_weight, conv_in_bias, gain_in,
    up_weight, up_bias, gain_up, out_weight, out_bias,
):
    num_dev = lax.axis_size("seq")
    dev_index = lax.axis_index("seq")
    frames, feat, tok_total = hidden.shape
    tile = tok_total // num_dev
    rows_dev = tile // TOK_W
    patch = head_weight.shape[0]
    lat_ch = patch // 4
    scaled = head_weight * (1.0 + mod_scale)
    sums = jnp.sum(scaled.reshape(patch, num_dev, feat), axis=2)
    base = jnp.sum(head_weight * mod_shift, axis=1) + head_bias

    mine = lax.dynamic_slice_in_dim(head_weight, dev_index * feat, feat, axis=1)
    mine = mine * (1.0 + lax.dynamic_slice_in_dim(mod_scale, dev_index * feat, feat))
    vmem = pl.BlockSpec(memory_space=pltpu.VMEM)
    sent = pl.pallas_call(
        functools.partial(head_kernel, num_dev),
        out_shape=jax.ShapeDtypeStruct((num_dev, tile + 8, frames * patch), F32),
        in_specs=[vmem, vmem],
        out_specs=vmem,
        compiler_params=pltpu.CompilerParams(vmem_limit_bytes=40 * 1024 * 1024),
    )(hidden, mine)
    got = lax.all_to_all(sent, "seq", split_axis=0, concat_axis=0, tiled=True)

    projected = pl.pallas_call(
        functools.partial(merge_kernel, feat, tile),
        out_shape=jax.ShapeDtypeStruct((frames, tile, patch), BF16),
        in_specs=[vmem] * 3,
        out_specs=vmem,
        compiler_params=pltpu.CompilerParams(vmem_limit_bytes=40 * 1024 * 1024),
    )(got, sums.T, base[None])
    projected = projected.reshape(frames, rows_dev, TOK_W, patch)

    forward = [(i, i + 1) for i in range(num_dev - 1)]
    backward = [(j, i) for i, j in forward]
    low = lax.ppermute(projected[:, -1:], "seq", forward)
    high = lax.ppermute(projected[:, :1], "seq", backward)
    rows = jnp.concatenate([low, projected, high], axis=1)
    latent = rows.reshape(frames, rows_dev + 2, TOK_W, 2, 2 * lat_ch).transpose(0, 1, 3, 2, 4)
    latent = latent.reshape(frames, 2 * rows_dev + 4, TOK_W, 2 * lat_ch)
    left = jnp.pad(latent[:, :, :-1, lat_ch:], ((0, 0), (0, 0), (1, 0), (0, 0)))
    right = jnp.pad(latent[:, :, 1:, :lat_ch], ((0, 0), (0, 0), (0, 1), (0, 0)))
    quad = jnp.concatenate([left, latent, right], axis=-1)
    out_rows = 2 * rows_dev + 2
    x1 = jnp.concatenate([quad[:, b : b + out_rows] for b in range(3)], axis=-1)
    return decode(x1, dev_index, num_dev, conv_in_weight, conv_in_bias, gain_in, up_weight, up_bias, gain_up, out_weight, out_bias)


def solution(mesh):
    placed = (P("grp", "seq", None), P(), P(), P(), P(), P(), P(), P(), P(), P(), P(), P(), P())
    return jax.shard_map(
        local, mesh=mesh, in_specs=placed, out_specs=P("grp", "seq", None, None), check_vma=False
    )
```

profile of v0, /device:TPU:13, one launch (start us, length us, event | category | flops | bytes accessed | tf_op | source)
XLA Modules:
  0.0 52.7 jit_solution(14118774584412655586)
XLA Ops:
  0.0 0.8 %dynamic-slice_add_fusion = f32[320]{0:T(512)S(1)} fusion(f32[5120]{0:T(1024)} %param.15, s32[]{:T(128)S(6)} %select_n.4), kind=kLoop, calls=%fused_computation.32 | loop fusion | flops 320 | bytes 2564 | tf_op jit(solution)/shard_map/add | solution.py:208
  0.8 1.0 %dynamic-slice_multiply_fusion.w_ref = f32[64,320]{1,0:T(8,128)S(1)} fusion(f32[64,5120]{1,0:T(8,128)} %param.16, s32[]{:T(128)S(6)} %select_n.4, f32[320]{0:T(512)S(1)} %dynamic-slice_add_fusion), kind=kLoop, calls=%fused_computation.30 | loop fusion | flops 20480 | bytes 165124 | tf_op jit(solution)/shard_map/mul | solution.py:208
  1.8 0.0 copy-start.1
  1.8 1.4 %copy-done.1 = bf16[2,320,1280]{2,1,0:T(8,128)(2,1)S(1)} copy-done((bf16[2,320,1280]{2,1,0:T(8,128)(2,1)S(1)}, bf16[2,320,1280]{2,1,0:T(8,128)(2,1)}, u32[]{:S(2)}) %copy-start.1) | copy-done | bytes 1638424
  3.2 2.3 %shard_map.127 = f32[16,88,128]{2,1,0:T(8,128)} custom-call(bf16[2,320,1280]{2,1,0:T(8,128)(2,1)S(1)} %copy-done.1, f32[64,320]{1,0:T(8,128)S(1)} %dynamic-slice_multiply_fusion.w_ref), custom_call_target="tpu_custom_call" | custom-call | tf_op jit(solution)/shard_map/pallas_call | solution.py:210
  5.5 6.6 %all-to-all-start = ((f32[16,88,128]{2,1,0:T(8,128)}), f32[16,88,128]{2,1,0:T(8,128)}, u32[]{:S(2)}, u32[]{:S(2)}) async-start(f32[16,88,128]{2,1,0:T(8,128)} %shard_map.127), calls=%async_computation | async-start | bytes 1441792 | tf_op jit(solution)/shard_map/all_to_all | solution.py:217
  12.2 0.2 convert_element_type.13
  12.4 0.1 fusion.8
  12.5 0.0 copy-start.9
  12.5 0.0 copy-start.11
  12.6 0.1 slice_add_fusion.1
  12.7 1.1 %copy-done.9 = f32[64,5120]{1,0:T(8,128)S(1)} copy-done((f32[64,5120]{1,0:T(8,128)S(1)}, f32[64,5120]{1,0:T(8,128)}, u32[]{:S(2)}) %copy-start.9) | copy-done | bytes 1310744
  13.9 1.3 %multiply_reduce_fusion = (f32[64]{0:T(128)S(1)}, f32[64,5120]{1,0:T(8,128)}) fusion(f32[64,5120]{1,0:T(8,128)S(1)} %copy-done.9, f32[5120]{0:T(1024)S(1)} %copy-done.11, f32[5120]{0:T(1024)S(1)} %broadcast_add_fusion), kind=kLoop, calls=%fused_computation.7 | loop fusion | flops 982976 | bytes 2662656 | tf_op jit(solution)/shard_map/reduce_sum | solution.py:205
  15.2 1.5 %maximum_bitcast_fusion = (f32[1,2,3,384,192]{3,4,2,1,0:T(8,128)S(1)}, f32[1,2,3,384,192]{3,4,2,1,0:T(8,128)}) fusion(f32[1,3,384,192]{2,3,1,0:T(8,128)S(1)} %get-tuple-element.9, f32[1,3,384,192]{2,3,1,0:T(8,128)S(1)} %get-tuple-element.11, f32[1,3,384,192]{2,3,1,0:T(8,128)S(1)} %get-tuple-element.12, f32[1,3,384,192]{2,3,1,0:T(8,128)S(1)} %get-tuple-element.10), kind=kLoop, calls=%fused_computation.5 | loop fusion | flops 884736 | bytes 7077888 | tf_op jit(solution)/shard_map/stack | solution.py:117
  16.7 1.7 %reshape.28 = f32[64,16,320]{2,1,0:T(8,128)S(1)} reshape(f32[64,5120]{1,0:T(8,128)} %get-tuple-element.14) | data formatting | bytes 2621440 | tf_op jit(solution)/shard_map/reshape | solution.py:204
  18.4 0.2 reduce_sum.18
  18.7 0.1 copy.23
  18.7 2.0 %add_convert_fusion.1 = (bf16[2,2,1,384,192]{3,4,2,1,0:T(8,128)(2,1)S(1)}, bf16[2,2,1,384,192]{3,4,2,1,0:T(8,128)(2,1)S(1)}) fusion(f32[1,2,3,384,192]{3,4,2,1,0:T(8,128)} %get-tuple-element.25, f32[1,2,3,384,192]{3,4,2,1,0:T(8,128)S(1)} %get-tuple-element.24), kind=kLoop, calls=%fused_computation.17 | loop fusion | flops 2359296 | bytes 4718592 | tf_op jit(solution)/shard_map/convert.7
  20.7 0.2 copy-done.5
  20.9 0.2 fusion.6
  21.1 0.1 pad_maximum_fusion.2
  21.3 1.6 %copy.25 = bf16[2,2,2,384,192]{4,3,2,1,0:T(8,128)(2,1)} copy(bf16[2,2,2,384,192]{3,4,2,1,0:T(8,128)(2,1)S(1)} %pad_maximum_fusion.2) | data formatting | bytes 2359296 | tf_op jit(solution)/shard_map/stack | solution.py:122
  22.9 0.1 pad_maximum_fusion.3
  23.1 1.6 %copy.26 = bf16[2,2,2,384,192]{4,3,2,1,0:T(8,128)(2,1)} copy(bf16[2,2,2,384,192]{3,4,2,1,0:T(8,128)(2,1)S(1)} %pad_maximum_fusion.3) | data formatting | bytes 2359296 | tf_op jit(solution)/shard_map/stack | solution.py:123
  24.7 1.2 %slice-done = bf16[2,3,3,192,96]{4,3,2,1,0:T(8,128)(2,1)S(1)} async-done(((bf16[3,3,3,192,96]{4,3,2,1,0:T(8,128)(2,1)}), bf16[2,3,3,192,96]{4,3,2,1,0:T(8,128)(2,1)S(1)}, s32[]{:S(2)}) %slice-start) | async-done | bytes 663576 | tf_op jit(solution)/shard_map/slice | solution.py:128
  25.8 0.3 pad_slice_fusion.5
  26.1 1.2 %pad_maximum_fusion.4.w3_ref = bf16[3,768,256]{2,1,0:T(8,128)(2,1)} fusion(bf16[3,768,128]{2,1,0:T(8,128)(2,1)S(1)} %bitcast.32, bf16[3,768,128]{2,1,0:T(8,128)(2,1)S(1)} %bitcast.31), kind=kLoop, calls=%fused_computation.15 | loop fusion | flops 2359296 | bytes 2359296 | tf_op jit(solution)/shard_map/concatenate | solution.py:129
  27.3 0.0 copy-done.8
  27.3 0.9 %copy-done.7 = bf16[2,2,2,384,192]{4,3,2,1,0:T(8,128)(2,1)S(1)} copy-done((bf16[2,2,2,384,192]{4,3,2,1,0:T(8,128)(2,1)S(1)}, bf16[2,2,2,384,192]{4,3,2,1,0:T(8,128)(2,1)}, u32[]{:S(2)}) %copy-start.7) | copy-done | bytes 1179672
  28.2 0.6 %pad_maximum_fusion.w2_ref = bf16[2,2,2,768,192]{4,3,2,1,0:T(8,128)(2,1)S(1)} fusion(bf16[2,2,1,768,192]{4,3,2,1,0:T(8,128)(2,1)S(1)} %bitcast.28, bf16[2,2,1,768,192]{4,3,2,1,0:T(8,128)(2,1)S(1)} %bitcast.27), kind=kLoop, calls=%fused_computation.4 | loop fusion | flops 1179648 | bytes 4718592 | tf_op jit(solution)/shard_map/stack | solution.py:120
  28.8 0.0 copy-done.14
  28.9 1.2 %all-to-all-done.got_ref = f32[16,88,128]{2,1,0:T(8,128)} async-done(((f32[16,88,128]{2,1,0:T(8,128)}), f32[16,88,128]{2,1,0:T(8,128)}, u32[]{:S(2)}, u32[]{:S(2)}) %all-to-all-start) | async-done | bytes 720928 | tf_op jit(solution)/shard_map/all_to_all | solution.py:217
  30.1 1.6 %shard_map.128 = bf16[2,80,64]{2,1,0:T(8,128)(2,1)S(1)} custom-call(f32[16,88,128]{2,1,0:T(8,128)} %all-to-all-done.got_ref, f32[16,64]{1,0:T(8,128)S(1)} %bitcast.24, f32[1,64]{1,0:T(1,128)S(1)} %add_bitcast_fusion.base_ref), custom_call_target="tpu_custom_call" | custom-call | tf_op jit(solution)/shard_map/pallas_call | solution.py:219
  31.7 3.6 %collective-permute-start = (bf16[2,1,80,64]{3,2,0,1:T(8,128)(2,1)S(1)}, bf16[2,1,80,64]{3,2,0,1:T(8,128)(2,1)S(1)}, u32[]{:S(2)}, u32[]{:S(2)}) collective-permute-start(bf16[2,1,80,64]{3,2,0,1:T(8,128)(2,1)S(1)} %bitcast.21), channel_id=1, source_target_pairs={{0,1},{1,2},{2,3},{3,4},{4,5},{5,6},{6,7},{7,8},{8,9},{9,10},{10,1... | collective-permute-start | bytes 61448 | tf_op jit(solution)/shard_map/ppermute | solution.py:230
  35.3 2.1 %collective-permute-start.1 = (bf16[2,1,80,64]{3,2,0,1:T(8,128)(2,1)S(1)}, bf16[2,1,80,64]{3,2,0,1:T(8,128)(2,1)S(1)}, u32[]{:S(2)}, u32[]{:S(2)}) collective-permute-start(bf16[2,1,80,64]{3,2,0,1:T(8,128)(2,1)S(1)} %bitcast.22), channel_id=1, source_target_pairs={{1,0},{2,1},{3,2},{4,3},{5,4},{6,5},{7,6},{8,7},{9,8},{10,9},{11,1... | collective-permute-start | bytes 61448 | tf_op jit(solution)/shard_map/ppermute | solution.py:231
  37.5 4.0 %collective-permute-done.1 = bf16[2,1,80,64]{3,2,0,1:T(8,128)(2,1)S(1)} collective-permute-done((bf16[2,1,80,64]{3,2,0,1:T(8,128)(2,1)S(1)}, bf16[2,1,80,64]{3,2,0,1:T(8,128)(2,1)S(1)}, u32[]{:S(2)}, u32[]{:S(2)}) %collective-permute-start.1) | collective-permute-done | bytes 20512 | tf_op jit(solution)/shard_map/ppermute | solution.py:231
  41.6 0.1 fusion.11
  41.7 0.1 pad_maximum_fusion.6
  41.8 0.2 fusion.10
  42.0 0.0 copy-start.2
  42.0 0.0 copy-start.3
  42.0 0.0 copy-start.4
  42.0 0.3 fusion.4
  42.3 0.1 fusion.9
  42.4 0.2 pad_maximum_fusion.5.x_ref
  42.5 0.7 %copy-done = bf16[3,768,256]{2,1,0:T(8,128)(2,1)S(1)} copy-done((bf16[3,768,256]{2,1,0:T(8,128)(2,1)S(1)}, bf16[3,768,256]{2,1,0:T(8,128)(2,1)}, u32[]{:S(2)}) %copy-start) | copy-done | bytes 1179672
  43.2 0.1 copy-done.2
  43.3 9.4 %shard_map.129 = bf16[8,96,320]{2,1,0:T(8,128)(2,1)} custom-call(s32[1]{0:T(128)} %bitcast.pos_ref, bf16[2,4,80,192]{3,2,1,0:T(8,128)(2,1)S(1)} %pad_maximum_fusion.5.x_ref, bf16[3,3,3,16,384]{4,3,2,1,0:T(8,128)(2,1)S(1)} %copy-done.2, f32[1,384]{1,0:T(1,128)S(1)} %broadcast_in_dim.26.b1_ref, f32[1,384]{1,0:T(1,128)S(1)} %broadcast_in_dim.27.g1_ref, ...), custom_call_target="tpu_custom_call" | custom-call | tf_op jit(solution)/shard_map/pallas_call | solution.py:133
  (27 shorter events, 0.1 us)
Async XLA Ops:
  1.8 1.4 %copy-start.1 = (bf16[2,320,1280]{2,1,0:T(8,128)(2,1)S(1)}, bf16[2,320,1280]{2,1,0:T(8,128)(2,1)}, u32[]{:S(2)}) copy-start(bf16[2,320,1280]{2,1,0:T(8,128)(2,1)} %x_ref.1) | copy-start | bytes 4915204
  5.5 6.7 %copy-start.10 = (f32[5120]{0:T(1024)S(1)}, f32[5120]{0:T(1024)}, u32[]{:S(2)}) copy-start(f32[5120]{0:T(1024)} %param.15) | copy-start | bytes 61444
  5.5 6.7 %copy-start.6 = (bf16[3,3,384,192]{2,3,1,0:T(8,128)(2,1)S(1)}, bf16[3,3,384,192]{2,3,1,0:T(8,128)(2,1)}, u32[]{:S(2)}) copy-start(bf16[3,3,384,192]{2,3,1,0:T(8,128)(2,1)} %param.21) | copy-start | bytes 3981316
  5.5 24.6 %all-to-all-start = ((f32[16,88,128]{2,1,0:T(8,128)}), f32[16,88,128]{2,1,0:T(8,128)}, u32[]{:S(2)}, u32[]{:S(2)}) async-start(f32[16,88,128]{2,1,0:T(8,128)} %shard_map.127), calls=%async_computation | async-start | bytes 1441792 | tf_op jit(solution)/shard_map/all_to_all | solution.py:217
  12.5 1.3 %copy-start.9 = (f32[64,5120]{1,0:T(8,128)S(1)}, f32[64,5120]{1,0:T(8,128)}, u32[]{:S(2)}) copy-start(f32[64,5120]{1,0:T(8,128)} %param.16) | copy-start | bytes 3932164
  12.5 1.3 %copy-start.11 = (f32[5120]{0:T(1024)S(1)}, f32[5120]{0:T(1024)}, u32[]{:S(2)}) copy-start(f32[5120]{0:T(1024)} %param.14) | copy-start | bytes 61444
  18.7 2.2 %copy-start.5 = (f32[1,2,3,384,192]{3,4,2,1,0:T(8,128)S(1)}, f32[1,2,3,384,192]{3,4,2,1,0:T(8,128)}, u32[]{:S(2)}) copy-start(f32[1,2,3,384,192]{3,4,2,1,0:T(8,128)} %get-tuple-element.25) | copy-start | bytes 5308420
  24.7 1.2 %slice-start = ((bf16[3,3,3,192,96]{4,3,2,1,0:T(8,128)(2,1)}), bf16[2,3,3,192,96]{4,3,2,1,0:T(8,128)(2,1)S(1)}, s32[]{:S(2)}) async-start(bf16[3,3,3,192,96]{4,3,2,1,0:T(8,128)(2,1)} %param.24), calls=%async_computation.1 | async-start | bytes 1769472 | tf_op jit(solution)/shard_map/slice | solution.py:128
  25.8 1.5 %copy-start.8 = (bf16[2,2,2,384,192]{4,3,2,1,0:T(8,128)(2,1)S(1)}, bf16[2,2,2,384,192]{4,3,2,1,0:T(8,128)(2,1)}, u32[]{:S(2)}) copy-start(bf16[2,2,2,384,192]{4,3,2,1,0:T(8,128)(2,1)} %copy.26) | copy-start | bytes 3538948
  26.1 2.1 %copy-start.7 = (bf16[2,2,2,384,192]{4,3,2,1,0:T(8,128)(2,1)S(1)}, bf16[2,2,2,384,192]{4,3,2,1,0:T(8,128)(2,1)}, u32[]{:S(2)}) copy-start(bf16[2,2,2,384,192]{4,3,2,1,0:T(8,128)(2,1)} %copy.25) | copy-start | bytes 3538948
  28.2 0.7 %copy-start.14 = (f32[64]{0:T(128)S(1)}, f32[64]{0:T(128)}, u32[]{:S(2)}) copy-start(f32[64]{0:T(128)} %param.17) | copy-start | bytes 772
  28.2 9.2 %copy-start.15 = (f32[96]{0:T(128)S(1)}, f32[96]{0:T(128)}, u32[]{:S(2)}) copy-start(f32[96]{0:T(128)} %param.25) | copy-start | bytes 1156
  28.2 9.2 %copy-start.12 = (f32[384]{0:T(512)S(1)}, f32[384]{0:T(512)}, u32[]{:S(2)}) copy-start(f32[384]{0:T(512)} %param.19) | copy-start | bytes 4612
  28.2 9.3 %copy-start.13 = (f32[384]{0:T(512)S(1)}, f32[384]{0:T(512)}, u32[]{:S(2)}) copy-start(f32[384]{0:T(512)} %param.20) | copy-start | bytes 4612
  31.7 5.8 %collective-permute-start = (bf16[2,1,80,64]{3,2,0,1:T(8,128)(2,1)S(1)}, bf16[2,1,80,64]{3,2,0,1:T(8,128)(2,1)S(1)}, u32[]{:S(2)}, u32[]{:S(2)}) collective-permute-start(bf16[2,1,80,64]{3,2,0,1:T(8,128)(2,1)S(1)} %bitcast.21), channel_id=1, source_target_pairs={{0,1},{1,2},{2,3},{3,4},{4,5},{5,6},{6,7},{7,8},{8,9},{9,10},{10,1... | collective-permute-start | bytes 61448 | tf_op jit(solution)/shard_map/ppermute | solution.py:230
  35.3 6.2 %collective-permute-start.1 = (bf16[2,1,80,64]{3,2,0,1:T(8,128)(2,1)S(1)}, bf16[2,1,80,64]{3,2,0,1:T(8,128)(2,1)S(1)}, u32[]{:S(2)}, u32[]{:S(2)}) collective-permute-start(bf16[2,1,80,64]{3,2,0,1:T(8,128)(2,1)S(1)} %bitcast.22), channel_id=1, source_target_pairs={{1,0},{2,1},{3,2},{4,3},{5,4},{6,5},{7,6},{8,7},{9,8},{10,9},{11,1... | collective-permute-start | bytes 61448 | tf_op jit(solution)/shard_map/ppermute | solution.py:231
  41.9 1.3 %copy-start = (bf16[3,768,256]{2,1,0:T(8,128)(2,1)S(1)}, bf16[3,768,256]{2,1,0:T(8,128)(2,1)}, u32[]{:S(2)}) copy-start(bf16[3,768,256]{2,1,0:T(8,128)(2,1)} %pad_maximum_fusion.4.w3_ref) | copy-start | bytes 3538948
  42.0 1.3 %copy-start.2 = (bf16[3,3,3,16,384]{4,3,2,1,0:T(8,128)(2,1)S(1)}, bf16[3,3,3,16,384]{4,3,2,1,0:T(8,128)(2,1)}, u32[]{:S(2)}) copy-start(bf16[3,3,3,16,384]{4,3,2,1,0:T(8,128)(2,1)} %w1_ref.1) | copy-start | bytes 995332
  42.0 1.3 %copy-start.3 = (f32[192]{0:T(256)S(1)}, f32[192]{0:T(256)}, u32[]{:S(2)}) copy-start(f32[192]{0:T(256)} %param.22) | copy-start | bytes 2308
  42.0 1.3 %copy-start.4 = (f32[192]{0:T(256)S(1)}, f32[192]{0:T(256)}, u32[]{:S(2)}) copy-start(f32[192]{0:T(256)} %param.23) | copy-start | bytes 2308
where the time goes:
time: 53.2 us; the launch traced here: 52.7 us
  Pallas kernels  13.3 us (25%)
  starting transfers between devices  12.4 us (23%)
  local copies, waits for them, and re-layouts  11.5 us (22%)
  other arithmetic  9.95 us (19%)
  waiting for transfers between devices  5.27 us (10%)
    pallas_call x1, Pallas kernels, decode(): pl.pallas_call(functools.partial(conv_kernel, num_dev, lat_rows, (c1, c2,...  9.42 us
    all_to_all x1, starting transfers between devices, local(): got = lax.all_to_all(sent, 'seq', split_axis=0, concat_axis=0, tiled=True)  6.65 us
    unnamed x32, local copies, waits for them, and re-layouts  4.54 us
    ppermute x1, waiting for transfers between devices, local(): high = lax.ppermute(projected[:, :1], 'seq', backward)  4.04 us
    ppermute x1, starting transfers between devices, local(): low = lax.ppermute(projected[:, -1:], 'seq', forward)  3.61 us
    pallas_call x1, Pallas kernels, local(): pl.pallas_call(functools.partial(head_kernel, num_dev), out_shape=jax.Sha...  2.31 us
    another operation x2, other arithmetic  2.2 us
    ppermute x1, starting transfers between devices, local(): high = lax.ppermute(projected[:, :1], 'seq', backward)  2.1 us
  transfers between devices with their start and end apart: 3, of which 2 were waited for; matrix products, arithmetic and copies ran while one was open for 25% of the time, Pallas kernels for 0%

commit v1 on v0

v1 whole, which is shorter than its diff:
```python
import functools
import math

import jax
import jax.numpy as jnp
from jax import lax
from jax.experimental import pallas as pl
from jax.experimental.pallas import tpu as pltpu
from jax.sharding import PartitionSpec as P

TOK_W = 80
HIGH = lax.Precision.HIGHEST
F32 = jnp.float32
BF16 = jnp.bfloat16


def rms_silu(values, gain_vec):
    squares = jnp.mean(values * values, axis=-1, keepdims=True)
    normed = values * lax.rsqrt(squares + 1e-06) * gain_vec
    return normed * jax.nn.sigmoid(normed)


def shift_cols(values, step):
    count = values.shape[0]
    col = lax.broadcasted_iota(jnp.int32, (count, 1), 0) % TOK_W
    if step > 0:
        return jnp.where(col == 0, 0.0, pltpu.roll(values, 1, 0))
    return jnp.where(col == TOK_W - 1, 0.0, pltpu.roll(values, count - 1, 0))


def conv_kernel(num_dev, lat_rows, chans, x_ref, w1_ref, b1_ref, g1_ref, w2_ref, b2_ref, g2_ref,
                w3_ref, b3_ref, out_ref, act1, act2, res, w1s):
    c1, c2, c3 = chans
    ch = w1_ref.shape[3]
    blank = jnp.zeros((ch, c1), BF16)
    for a in range(2):
        for b in range(3):
            for j in range(4):
                rows = slice((4 * b + j) * ch, (4 * b + j + 1) * ch)
                w1s[a, rows, 0:c1] = w1_ref[a + 1, b, j] if j < 3 else blank
                w1s[a, rows, c1 : 2 * c1] = w1_ref[a + 1, b, j - 1] if j > 0 else blank
    dev = lax.axis_index("seq")
    rows1 = lat_rows + 2
    m1 = rows1 * TOK_W
    rows2 = lat_rows + 1
    m2 = rows2 * TOK_W
    rows3 = 2 * lat_rows
    m3 = rows3 * TOK_W

    def inside(count, first, step, total):
        row = lax.broadcasted_iota(jnp.int32, (count, 1), 0) // TOK_W * step + first
        return (row >= 0) & (row < total)

    keep1 = inside(m1, dev * lat_rows - 1, 1, num_dev * lat_rows)
    for frame in range(2):
        x_now = x_ref[frame].reshape(m1, x_ref.shape[-1])
        pre = jnp.dot(x_now, w1s[1], preferred_element_type=F32)
        if frame == 1:
            x_old = x_ref[0].reshape(m1, x_ref.shape[-1])
            pre = pre + jnp.dot(x_old, w1s[0], preferred_element_type=F32)
        for r in range(2):
            val = rms_silu(pre[:, r * c1 : (r + 1) * c1] + b1_ref[...], g1_ref[...])
            val = jnp.where(keep1, val, 0.0)
            edge = shift_cols(val, 1) if r == 1 else shift_cols(val, -1)
            spot = 0 if r == 1 else 3
            act1[frame, :, :, (r + 1) * c1 : (r + 2) * c1] = val.astype(BF16).reshape(rows1, TOK_W, c1)
            act1[frame, :, :, spot * c1 : (spot + 1) * c1] = edge.astype(BF16).reshape(rows1, TOK_W, c1)

    start = (0, 1, 1, 2)
    for p in range(2):
        first = 0 if p == 0 else -1
        keep2 = inside(m2, 2 * dev * lat_rows + first, 2, 2 * num_dev * lat_rows)
        for frame in range(2):
            for s in range(4):
                q = s % 2
                lanes = slice(start[s] * c1, (start[s] + 2) * c1)
                top = act1[frame, 0:rows2, :, lanes].reshape(m2, 2 * c1)
                low = act1[frame, 1 : rows2 + 1, :, lanes].reshape(m2, 2 * c1)
                pre = jnp.dot(top, w2_ref[p, 0, q], preferred_element_type=F32)
                pre = pre + jnp.dot(low, w2_ref[p, 1, q], preferred_element_type=F32)
                val = rms_silu(pre + b2_ref[...], g2_ref[...])
                val = jnp.where(keep2, val, 0.0)
                val = jnp.concatenate([val, jnp.zeros((m2, 256 - c2), F32)], axis=1)
                pieces = [(s + 1, val)]
                if s == 3:
                    pieces.append((0, shift_cols(val, 1)))
                if s == 0:
                    pieces.append((5, shift_cols(val, -1)))
                for spot, piece in pieces:
                    piece = piece.astype(BF16).reshape(rows2, TOK_W, 256)
                    for i in range(rows2):
                        act2[frame, 2 * i + 1 - p, :, spot * 256 : (spot + 1) * 256] = piece[i]

    for s in range(4):
        lanes = slice(s * 256, (s + 3) * 256)
        old = None
        new = None
        for b in range(3):
            before = act2[0, b : b + rows3, :, lanes].reshape(m3, 768)
            after = act2[1, b : b + rows3, :, lanes].reshape(m3, 768)
            one = jnp.dot(before, w3_ref[b], preferred_element_type=F32)
            two = jnp.dot(after, w3_ref[b, :, 0:128], preferred_element_type=F32)
            old = one if old is None else old + one
            new = two if new is None else new + two
        res[pl.ds(s, m3, stride=4), :] = old[:, 0:128] + b3_ref[...]
        res[pl.ds(4 * m3 + s, m3, stride=4), :] = old[:, 128:256] + new + b3_ref[...]
    width = 4 * TOK_W
    for i in range(2 * rows3):
        out_ref[i] = jnp.transpose(res[i * width : (i + 1) * width, :])[0:c3].astype(BF16)


def exchange_kernel(num_dev, x_hbm, w_hbm, scale_hbm, shift_hbm, bias_hbm, up_hbm, outw_hbm, b1_hbm, g1_hbm, b3_hbm,
                    x1_ref, w2_ref, w3_ref, b1_ref, g1_ref, b3_ref,
                    xbuf, wbuf, modbuf, upbuf, outbuf, biasbuf, b1buf, g1buf, b3buf, send, stat, got, gotstat, rows,
                    in_sem, weight_sem, send_sem, recv_sem, stat_send, stat_recv, halo_send, halo_recv):
    frames, feat, total = x_hbm.shape
    patch, width = w_hbm.shape
    tile = total // num_dev
    half = tile // 2
    c1, c2 = up_hbm.shape[3], up_hbm.shape[2]
    c3 = outw_hbm.shape[4]
    me = lax.axis_index("seq")

    def peer(step):
        spot = me
        bit = 1
        while bit < num_dev:
            if step & bit:
                spot = spot + (1 - 2 * ((me // bit) % 2)) * bit
            bit *= 2
        return spot

    window = wbuf.shape[1]
    begin = jnp.minimum((me * feat) // 128 * 128, width - window)
    lanes = pl.ds(pl.multiple_of(begin, 128), window)
    loads = [
        pltpu.make_async_copy(w_hbm.at[:, lanes], wbuf, in_sem.at[0]),
        pltpu.make_async_copy(scale_hbm.at[:, lanes], modbuf.at[0], in_sem.at[1]),
        pltpu.make_async_copy(shift_hbm.at[:, lanes], modbuf.at[1], in_sem.at[2]),
    ]
    planes = [pltpu.make_async_copy(x_hbm.at[f], xbuf.at[f], in_sem.at[3 + f]) for f in range(frames)]
    weights = [
        pltpu.make_async_copy(up_hbm, upbuf, weight_sem.at[0]),
        pltpu.make_async_copy(outw_hbm.at[pl.ds(1, 2)], outbuf, weight_sem.at[1]),
        pltpu.make_async_copy(bias_hbm, biasbuf, weight_sem.at[2]),
        pltpu.make_async_copy(b1_hbm, b1buf, weight_sem.at[3]),
        pltpu.make_async_copy(g1_hbm, g1buf, weight_sem.at[4]),
        pltpu.make_async_copy(b3_hbm, b3buf, weight_sem.at[5]),
    ]
    for copy in loads + planes + weights:
        copy.start()

    barrier = pltpu.get_barrier_semaphore()
    for step in range(1, num_dev):
        pl.semaphore_signal(barrier, inc=1, device_id={"seq": peer(step)})

    for copy in loads:
        copy.wait()
    turn = lax.rem(begin - me * feat + window, window)
    plain = pltpu.roll(wbuf[...], turn, 1)[:, 0:feat]
    scale = pltpu.roll(jnp.broadcast_to(modbuf[0], (8, window)), turn, 1)[0:1, 0:feat]
    shift = pltpu.roll(jnp.broadcast_to(modbuf[1], (8, window)), turn, 1)[0:1, 0:feat]
    weight = plain * (1.0 + scale)
    high = weight.astype(BF16)
    low = (weight - high.astype(F32)).astype(BF16)
    stack = jnp.concatenate([high, low], axis=0)
    sums = jnp.sum(high.astype(F32) + low.astype(F32), axis=1, keepdims=True)
    base = jnp.sum(plain * shift, axis=1, keepdims=True)
    both = jnp.concatenate([sums, base], axis=0)
    line = jnp.transpose(jnp.broadcast_to(both, (2 * patch, 8)))

    def messages(f):
        out = []
        for step in range(num_dev - 1, 0, -1):
            dest = peer(step)
            out.append(pltpu.make_async_remote_copy(
                src_ref=stat.at[f, dest], dst_ref=gotstat.at[f, me], send_sem=stat_send.at[f, dest],
                recv_sem=stat_recv.at[f, me], device_id={"seq": dest}))
            out.append(pltpu.make_async_remote_copy(
                src_ref=send.at[f, dest], dst_ref=got.at[f, me], send_sem=send_sem.at[f, dest],
                recv_sem=recv_sem.at[f, me], device_id={"seq": dest}))
        return out

    def arrivals(f):
        out = []
        for step in range(num_dev - 1, 0, -1):
            origin = peer(step)
            out.append(pltpu.make_async_remote_copy(
                src_ref=stat.at[f, origin], dst_ref=gotstat.at[f, origin], send_sem=stat_send.at[f, origin],
                recv_sem=stat_recv.at[f, origin], device_id={"seq": origin}))
            out.append(pltpu.make_async_remote_copy(
                src_ref=send.at[f, origin], dst_ref=got.at[f, origin], send_sem=send_sem.at[f, origin],
                recv_sem=recv_sem.at[f, origin], device_id={"seq": origin}))
        return out

    for f in range(frames):
        planes[f].wait()
        block = xbuf[f]
        full = jnp.dot(stack, block, preferred_element_type=F32)
        values = block.astype(F32)
        mean = jnp.sum(values, axis=0, keepdims=True) * (1.0 / feat)
        centred = values - mean
        spread = jnp.sum(centred * centred, axis=0, keepdims=True)
        part = full[:patch] + full[patch:] - sums * mean
        flat = jnp.transpose(part).reshape(num_dev, 2, half, patch)
        packed = jnp.concatenate([flat[:, 0], flat[:, 1]], axis=-1)
        send[f] = packed.astype(BF16)
        for i in range(num_dev):
            stat[f, i, 0:1, 0:tile] = mean[:, i * tile : (i + 1) * tile]
            stat[f, i, 1:2, 0:tile] = spread[:, i * tile : (i + 1) * tile]
            stat[f, i, 2:3, :] = line[0:1]
            stat[f, i, 3:8, :] = jnp.zeros((5, 128), F32)
        if f == 0:
            pl.semaphore_wait(barrier, num_dev - 1)
        for copy in messages(f):
            copy.start()
        got[f, me] = send[f, me]
        gotstat[f, me] = stat[f, me]

    for copy in weights:
        copy.wait()
    taps = [[jnp.transpose(upbuf[r, c].astype(F32)) for c in range(3)] for r in range(3)]
    for p in range(2):
        for i in range(2):
            group = ((0,), (1, 2)) if p == 0 else ((0, 1), (2,))
            tall = [functools.reduce(lambda a, b: a + b, [taps[r][c] for r in group[i]]) for c in range(3)]
            for q in range(2):
                first = tall[0] if q == 0 else tall[0] + tall[1]
                second = tall[1] + tall[2] if q == 0 else tall[2]
                w2_ref[p, i, q, 0:c1, :] = first.astype(BF16)
                w2_ref[p, i, q, c1 : 2 * c1, :] = second.astype(BF16)
    w3_ref[...] = jnp.zeros(w3_ref.shape, BF16)
    b1_ref[...] = b1buf[...].reshape(1, c1)
    g1_ref[...] = g1buf[...].reshape(1, c1)
    b3_ref[...] = jnp.concatenate([b3buf[...].reshape(1, c3), jnp.zeros((1, 128 - c3), F32)], axis=1)
    for b in range(3):
        for e in range(3):
            w3_ref[b, e * 256 : e * 256 + c2, 0:c3] = outbuf[1, b, e]
            w3_ref[b, e * 256 : e * 256 + c2, 128 : 128 + c3] = outbuf[0, b, e]

    def to_next(f):
        return pltpu.make_async_remote_copy(
            src_ref=rows.at[f, 1], dst_ref=rows.at[f, 0], send_sem=halo_send.at[f, 0],
            recv_sem=halo_recv.at[f, 0], device_id={"seq": lax.rem(me + 1, num_dev)})

    def to_last(f):
        return pltpu.make_async_remote_copy(
            src_ref=rows.at[f, 1], dst_ref=rows.at[f, 2], send_sem=halo_send.at[f, 1],
            recv_sem=halo_recv.at[f, 1], device_id={"seq": lax.rem(me + num_dev - 1, num_dev)})

    for f in range(frames):
        for copy in arrivals(f):
            copy.wait_recv()
        means = gotstat[f, :, 0, :]
        off = means - jnp.mean(means, axis=0, keepdims=True)
        spread = jnp.sum(gotstat[f, :, 1, :], axis=0, keepdims=True)
        var = (spread + feat * jnp.sum(off * off, axis=0, keepdims=True)) * (1.0 / width)
        scale = jnp.transpose(jnp.broadcast_to(lax.rsqrt(var + 1e-06), (8, 128)))[0:tile, 0:1]
        lines = gotstat[f, :, 2, :]
        fixed = jnp.dot(jnp.transpose(off), lines[:, 0:patch], precision=HIGH, preferred_element_type=F32)[0:tile]
        total_base = jnp.sum(lines, axis=0, keepdims=True)[:, patch:] + biasbuf[...].reshape(1, patch)
        summed = got[f, 0].astype(F32)
        for i in range(1, num_dev):
            summed = summed + got[f, i].astype(F32)
        summed = jnp.concatenate([summed[:, :patch], summed[:, patch:]], axis=0)
        done = ((summed + fixed) * scale + total_base).astype(BF16).astype(F32)
        rows[f, 1] = jnp.concatenate([done[:half], done[half:]], axis=1).astype(BF16)

        @pl.when(me < num_dev - 1)
        def _():
            to_next(f).start()

        @pl.when(me > 0)
        def _():
            to_last(f).start()

        @pl.when(me == 0)
        def _():
            rows[f, 0] = jnp.zeros((half, 128), BF16)

        @pl.when(me == num_dev - 1)
        def _():
            rows[f, 2] = jnp.zeros((half, 128), BF16)

    ch = patch // 4
    for f in range(frames):
        @pl.when(me > 0)
        def _():
            to_next(f).wait_recv()

        @pl.when(me < num_dev - 1)
        def _():
            to_last(f).wait_recv()

        quads = []
        col = lax.broadcasted_iota(jnp.int32, (tile, 1), 0)
        for h in range(3):
            pair = rows[f, h].astype(F32)
            token = jnp.concatenate([pair[:, :patch], pair[:, patch:]], axis=0)
            before = jnp.where(col == 0, 0.0, pltpu.roll(token, 1, 0))
            after = jnp.where(col == tile - 1, 0.0, pltpu.roll(token, tile - 1, 0))
            for q in range(2):
                a = 2 * q * ch
                quads.append(jnp.concatenate(
                    [before[:, a + ch : a + 2 * ch], token[:, a : a + 2 * ch], after[:, a : a + ch]], axis=1))
        for i in range(4):
            x1_ref[f, i] = jnp.concatenate(quads[i : i + 3], axis=1).astype(BF16)

    for f in range(frames):
        for copy in messages(f):
            copy.wait_send()

        @pl.when(me < num_dev - 1)
        def _():
            to_next(f).wait_send()

        @pl.when(me > 0)
        def _():
            to_last(f).wait_send()


def local(
    hidden, mod_shift, mod_scale, head_weight, head_bias, conv_in_weight, conv_in_bias, gain_in,
    up_weight, up_bias, gain_up, out_weight, out_bias,
):
    num_dev = lax.axis_size("seq")
    frames, feat, tok_total = hidden.shape
    tile = tok_total // num_dev
    rows_dev = tile // TOK_W
    patch, width = head_weight.shape
    lat_ch, c1 = conv_in_weight.shape[3:]
    c2, c3 = out_weight.shape[3:]
    lat_rows = 2 * rows_dev
    window = min(width, (feat + 255 - math.gcd(feat, 128)) // 128 * 128)
    vmem = pl.BlockSpec(memory_space=pltpu.VMEM)
    hbm = pl.BlockSpec(memory_space=pltpu.HBM)
    half = tile // 2
    raw = (hidden, head_weight, mod_scale[None], mod_shift[None], head_bias,
           jnp.transpose(up_weight, (0, 1, 3, 2)), out_weight, conv_in_bias, gain_in, out_bias)
    x1, w2, w3, b1, g1, b3 = pl.pallas_call(
        functools.partial(exchange_kernel, num_dev),
        out_shape=[
            jax.ShapeDtypeStruct((frames, lat_rows + 2, TOK_W, 12 * lat_ch), BF16),
            jax.ShapeDtypeStruct((2, 2, 2, 2 * c1, c2), BF16),
            jax.ShapeDtypeStruct((3, 768, 256), BF16),
            jax.ShapeDtypeStruct((1, c1), F32),
            jax.ShapeDtypeStruct((1, c1), F32),
            jax.ShapeDtypeStruct((1, 128), F32),
        ],
        in_specs=[hbm] * 10,
        out_specs=[vmem] * 6,
        scratch_shapes=[
            pltpu.VMEM((frames, feat, tok_total), BF16),
            pltpu.VMEM((patch, window), F32),
            pltpu.VMEM((2, 1, window), F32),
            pltpu.VMEM((3, 3, c2, c1), BF16),
            pltpu.VMEM((2, 3, 3, c2, c3), BF16),
            pltpu.VMEM((patch,), F32),
            pltpu.VMEM((c1,), F32),
            pltpu.VMEM((c1,), F32),
            pltpu.VMEM((c3,), F32),
            pltpu.VMEM((frames, num_dev, half, 2 * patch), BF16),
            pltpu.VMEM((frames, num_dev, 8, 128), F32),
            pltpu.VMEM((frames, num_dev, half, 2 * patch), BF16),
            pltpu.VMEM((frames, num_dev, 8, 128), F32),
            pltpu.VMEM((frames, 3, half, 2 * patch), BF16),
            pltpu.SemaphoreType.DMA((5,)),
            pltpu.SemaphoreType.DMA((6,)),
            pltpu.SemaphoreType.DMA((frames, num_dev)),
            pltpu.SemaphoreType.DMA((frames, num_dev)),
            pltpu.SemaphoreType.DMA((frames, num_dev)),
            pltpu.SemaphoreType.DMA((frames, num_dev)),
            pltpu.SemaphoreType.DMA((frames, 2)),
            pltpu.SemaphoreType.DMA((frames, 2)),
        ],
        compiler_params=pltpu.CompilerParams(
            vmem_limit_bytes=24 * 1024 * 1024, collective_id=0, has_side_effects=True),
    )(*[pltpu.with_memory_space_constraint(value, pltpu.HBM) for value in raw])
    cells = frames * 2 * lat_rows * 4 * TOK_W
    out = pl.pallas_call(
        functools.partial(conv_kernel, num_dev, lat_rows, (c1, c2, c3)),
        out_shape=jax.ShapeDtypeStruct((frames * 2 * lat_rows, c3, 4 * TOK_W), BF16),
        in_specs=[vmem] * 9,
        out_specs=vmem,
        scratch_shapes=[
            pltpu.VMEM((frames, lat_rows + 2, TOK_W, 4 * c1), BF16),
            pltpu.VMEM((frames, 2 * lat_rows + 2, TOK_W, 6 * 256), BF16),
            pltpu.VMEM((cells, 128), F32),
            pltpu.VMEM((2, 12 * lat_ch, 2 * c1), BF16),
        ],
        compiler_params=pltpu.CompilerParams(vmem_limit_bytes=24 * 1024 * 1024),
    )(x1, conv_in_weight, b1, g1,
      w2, up_bias[None], gain_up[None], w3, b3)
    return out.reshape(frames, 2 * lat_rows, c3, 4 * TOK_W).transpose(0, 1, 3, 2)


def solution(mesh):
    placed = (P("grp", "seq", None), P(), P(), P(), P(), P(), P(), P(), P(), P(), P(), P(), P())
    return jax.shard_map(
        local, mesh=mesh, in_specs=placed, out_specs=P("grp", "seq", None, None), check_vma=False
    )
```

time: 53.2 us -> 31.5 us (0.59)
  the two profiles are of different devices: /device:TPU:13 before, /device:TPU:1 now
where the time goes in v1:
time: 31.5 us; the launch traced here: 31.3 us
  Pallas kernels  31.3 us (99%)
    pallas_call x1, Pallas kernels, local(): pl.pallas_call(functools.partial(exchange_kernel, num_dev), out_shape=[ja...  22 us
    pallas_call x1, Pallas kernels, local(): pl.pallas_call(functools.partial(conv_kernel, num_dev, lat_rows, (c1, c2,...  9.28 us

profile of v1, /device:TPU:1, one launch (start us, length us, event | category | flops | bytes accessed | tf_op | source)
XLA Modules:
  0.0 31.3 jit_solution(6587405955593687722)
XLA Ops:
  0.0 0.0 copy-start
  0.0 0.0 copy-start.1
  0.0 0.0 copy-start.2
  0.0 22.0 %shard_map.127 = (bf16[2,4,80,192]{3,2,1,0:T(8,128)(2,1)S(1)}, bf16[2,2,2,768,192]{4,3,2,1,0:T(8,128)(2,1)S(1)}, bf16[3,768,256]{2,1,0:T(8,128)(2,1)S(1)}, f32[1...) custom-call(bf16[2,320,1280]{2,1,0:T(8,128)(2,1)} %x_hbm.1, f32[64,5120]{1,0:T(8,128)} %w_hbm.1, ...), custom_call_target="tpu_custom_call" | custom-call | tf_op jit(solution)/shard_map/pallas_call | solution.py:340
  22.0 0.0 copy-done
  22.0 0.0 copy-done.1
  22.0 0.0 copy-done.2
  22.0 9.3 %shard_map.128 = bf16[8,96,320]{2,1,0:T(8,128)(2,1)} custom-call(bf16[2,4,80,192]{3,2,1,0:T(8,128)(2,1)S(1)} %get-tuple-element.11.x_ref, bf16[3,3,3,16,384]{4,3,2,1,0:T(8,128)(2,1)S(1)} %copy-done, f32[1,384]{1,0:T(1,128)S(1)} %get-tuple-element.12.b1_ref, f32[1,384]{1,0:T(1,128)S(1)} %get-tuple-element.13.g1_ref, ...), custom_call_target="tpu_custom_call" | custom-call | tf_op jit(solution)/shard_map/pallas_call | solution.py:380
Async XLA Ops:
  0.0 22.0 %copy-start = (bf16[3,3,3,16,384]{4,3,2,1,0:T(8,128)(2,1)S(1)}, bf16[3,3,3,16,384]{4,3,2,1,0:T(8,128)(2,1)}, u32[]{:S(2)}) copy-start(bf16[3,3,3,16,384]{4,3,2,1,0:T(8,128)(2,1)} %w1_ref.1) | copy-start | bytes 995332
  0.0 22.0 %copy-start.1 = (f32[192]{0:T(256)S(1)}, f32[192]{0:T(256)}, u32[]{:S(2)}) copy-start(f32[192]{0:T(256)} %param.22) | copy-start | bytes 2308
  0.0 22.0 %copy-start.2 = (f32[192]{0:T(256)S(1)}, f32[192]{0:T(256)}, u32[]{:S(2)}) copy-start(f32[192]{0:T(256)} %param.23) | copy-start | bytes 2308

commit v2 on v1

v2 whole, which is shorter than its diff:
```python
import functools
import math

import jax
import jax.numpy as jnp
from jax import lax
from jax.experimental import pallas as pl
from jax.experimental.pallas import tpu as pltpu
from jax.sharding import PartitionSpec as P

TOK_W = 80
HIGH = lax.Precision.HIGHEST
F32 = jnp.float32
BF16 = jnp.bfloat16


def rms_silu(values, gain_vec):
    squares = jnp.mean(values * values, axis=-1, keepdims=True)
    normed = values * lax.rsqrt(squares + 1e-06) * gain_vec
    return normed * jax.nn.sigmoid(normed)


def shift_cols(values, step):
    count = values.shape[0]
    col = lax.broadcasted_iota(jnp.int32, (count, 1), 0) % TOK_W
    if step > 0:
        return jnp.where(col == 0, 0.0, pltpu.roll(values, 1, 0))
    return jnp.where(col == TOK_W - 1, 0.0, pltpu.roll(values, count - 1, 0))


def inside(count, first, step, total):
    row = lax.broadcasted_iota(jnp.int32, (count, 1), 0) // TOK_W * step + first
    return (row >= 0) & (row < total)


def stage_in(num_dev, dev, frame, x_ref, w1s, b1_ref, g1_ref, act1):
    rows1 = x_ref.shape[1]
    lat_rows = rows1 - 2
    c1 = g1_ref.shape[1]
    m1 = rows1 * TOK_W
    keep1 = inside(m1, dev * lat_rows - 1, 1, num_dev * lat_rows)
    x_now = x_ref[frame].reshape(m1, x_ref.shape[-1])
    pre = jnp.dot(x_now, w1s[1], preferred_element_type=F32)
    if frame == 1:
        x_old = x_ref[0].reshape(m1, x_ref.shape[-1])
        pre = pre + jnp.dot(x_old, w1s[0], preferred_element_type=F32)
    for r in range(2):
        val = rms_silu(pre[:, r * c1 : (r + 1) * c1] + b1_ref[...], g1_ref[...])
        val = jnp.where(keep1, val, 0.0)
        edge = shift_cols(val, 1) if r == 1 else shift_cols(val, -1)
        spot = 0 if r == 1 else 3
        act1[:, :, (r + 1) * c1 : (r + 2) * c1] = val.astype(BF16).reshape(rows1, TOK_W, c1)
        act1[:, :, spot * c1 : (spot + 1) * c1] = edge.astype(BF16).reshape(rows1, TOK_W, c1)


def stage_up(num_dev, dev, act1, w2_ref, b2_ref, g2_ref, act2):
    rows2 = act1.shape[0] - 1
    lat_rows = rows2 - 1
    c1 = act1.shape[2] // 4
    c2 = g2_ref.shape[1]
    m2 = rows2 * TOK_W
    start = (0, 1, 1, 2)
    for p in range(2):
        first = 0 if p == 0 else -1
        keep2 = inside(m2, 2 * dev * lat_rows + first, 2, 2 * num_dev * lat_rows)
        for s in range(4):
            q = s % 2
            lanes = slice(start[s] * c1, (start[s] + 2) * c1)
            top = act1[0:rows2, :, lanes].reshape(m2, 2 * c1)
            low = act1[1 : rows2 + 1, :, lanes].reshape(m2, 2 * c1)
            pre = jnp.dot(top, w2_ref[p, 0, q], preferred_element_type=F32)
            pre = pre + jnp.dot(low, w2_ref[p, 1, q], preferred_element_type=F32)
            val = rms_silu(pre + b2_ref[...], g2_ref[...])
            val = jnp.where(keep2, val, 0.0)
            val = jnp.concatenate([val, jnp.zeros((m2, 256 - c2), F32)], axis=1)
            pieces = [(s + 1, val)]
            if s == 3:
                pieces.append((0, shift_cols(val, 1)))
            if s == 0:
                pieces.append((5, shift_cols(val, -1)))
            for spot, piece in pieces:
                piece = piece.astype(BF16).reshape(rows2, TOK_W, 256)
                for i in range(rows2):
                    act2[2 * i + 1 - p, :, spot * 256 : (spot + 1) * 256] = piece[i]


def stage_out(act2, w3_ref, part, s):
    rows3 = act2.shape[0] - 2
    lanes = slice(s * 256, (s + 3) * 256)
    total = None
    for b in range(3):
        block = act2[b : b + rows3, :, lanes].reshape(rows3 * TOK_W, 768)
        one = jnp.dot(block, w3_ref[b, :, part], preferred_element_type=F32)
        total = one if total is None else total + one
    return total


def conv_kernel(num_dev, x_ref, w1s, b1_ref, g1_ref, w2_ref, b2_ref, g2_ref, w3_ref, res_ref, out_hbm,
                act1, act2, res, obuf, out_sem):
    dev = lax.axis_index("seq")
    rows3 = act2.shape[0] - 2
    m3 = rows3 * TOK_W
    c3 = obuf.shape[1]
    width = 4 * TOK_W
    copies = [pltpu.make_async_copy(obuf.at[i], out_hbm.at[i], out_sem.at[i]) for i in range(2 * rows3)]
    stage_in(num_dev, dev, 1, x_ref, w1s, b1_ref, g1_ref, act1)
    for i in range(rows3):
        obuf[i] = jnp.transpose(res_ref[i * width : (i + 1) * width, :])[0:c3].astype(BF16)
        copies[i].start()
    stage_up(num_dev, dev, act1, w2_ref, b2_ref, g2_ref, act2)
    for s in range(4):
        new = stage_out(act2, w3_ref, slice(0, 128), s)
        res[pl.ds(s, m3, stride=4), :] = new + res_ref[pl.ds(4 * m3 + s, m3, stride=4), :]
    for i in range(rows3):
        obuf[rows3 + i] = jnp.transpose(res[i * width : (i + 1) * width, :])[0:c3].astype(BF16)
        copies[rows3 + i].start()
    for copy in copies:
        copy.wait()


def exchange_kernel(num_dev, x_hbm, w_hbm, scale_hbm, shift_hbm, bias_hbm, up_hbm, outw_hbm, w1_hbm,
                    b1_hbm, g1_hbm, b2_hbm, g2_hbm, b3_hbm,
                    x1_ref, w1s, w2_ref, w3_ref, b1_ref, g1_ref, b2_ref, g2_ref, res_ref,
                    xbuf, wbuf, modbuf, upbuf, outbuf, w1buf, biasbuf, b1buf, g1buf, b2buf, g2buf, b3buf, act1, act2, pair, pairstat, gotpair, gotpairstat, send, stat, got, gotstat, rows,
                    in_sem, weight_sem, pair_send, pair_recv, send_sem, recv_sem, stat_send, stat_recv, halo_send, halo_recv):
    frames, feat, total = x_hbm.shape
    patch, width = w_hbm.shape
    tile = total // num_dev
    half = tile // 2
    c1, c2 = up_hbm.shape[3], up_hbm.shape[2]
    c3 = outw_hbm.shape[4]
    me = lax.axis_index("seq")

    def peer(step):
        spot = me
        bit = 1
        while bit < num_dev:
            if step & bit:
                spot = spot + (1 - 2 * ((me // bit) % 2)) * bit
            bit *= 2
        return spot

    window = wbuf.shape[1]
    begin = jnp.minimum((me * feat) // 128 * 128, width - window)
    lanes = pl.ds(pl.multiple_of(begin, 128), window)
    loads = [
        pltpu.make_async_copy(w_hbm.at[:, lanes], wbuf, in_sem.at[0]),
        pltpu.make_async_copy(scale_hbm.at[:, lanes], modbuf.at[0], in_sem.at[1]),
        pltpu.make_async_copy(shift_hbm.at[:, lanes], modbuf.at[1], in_sem.at[2]),
    ]
    planes = [pltpu.make_async_copy(x_hbm.at[f], xbuf.at[f], in_sem.at[3 + f]) for f in range(frames)]
    weights = [
        pltpu.make_async_copy(up_hbm, upbuf, weight_sem.at[0]),
        pltpu.make_async_copy(outw_hbm.at[pl.ds(1, 2)], outbuf, weight_sem.at[1]),
        pltpu.make_async_copy(bias_hbm, biasbuf, weight_sem.at[2]),
        pltpu.make_async_copy(b1_hbm, b1buf, weight_sem.at[3]),
        pltpu.make_async_copy(g1_hbm, g1buf, weight_sem.at[4]),
        pltpu.make_async_copy(b3_hbm, b3buf, weight_sem.at[5]),
        pltpu.make_async_copy(w1_hbm, w1buf, weight_sem.at[6]),
        pltpu.make_async_copy(b2_hbm, b2buf, weight_sem.at[7]),
        pltpu.make_async_copy(g2_hbm, g2buf, weight_sem.at[8]),
    ]
    for copy in loads + planes + weights:
        copy.start()

    barrier = pltpu.get_barrier_semaphore()
    for step in range(1, num_dev):
        pl.semaphore_signal(barrier, inc=1, device_id={"seq": peer(step)})

    for copy in loads:
        copy.wait()
    turn = lax.rem(begin - me * feat + window, window)
    plain = pltpu.roll(wbuf[...], turn, 1)[:, 0:feat]
    scale = pltpu.roll(jnp.broadcast_to(modbuf[0], (8, window)), turn, 1)[0:1, 0:feat]
    shift = pltpu.roll(jnp.broadcast_to(modbuf[1], (8, window)), turn, 1)[0:1, 0:feat]
    weight = plain * (1.0 + scale)
    high = weight.astype(BF16)
    low = (weight - high.astype(F32)).astype(BF16)
    stack = jnp.concatenate([high, low], axis=0)
    sums = jnp.sum(high.astype(F32) + low.astype(F32), axis=1, keepdims=True)
    base = jnp.sum(plain * shift, axis=1, keepdims=True)
    both = jnp.concatenate([sums, base], axis=0)
    line = jnp.transpose(jnp.broadcast_to(both, (2 * patch, 8)))

    core = lax.rem(me, 2)
    mine = me // 2
    pairs = num_dev // 2

    def swap(f):
        return [
            pltpu.make_async_remote_copy(
                src_ref=pairstat.at[f, 1 - core], dst_ref=gotpairstat.at[f], send_sem=pair_send.at[f, 0],
                recv_sem=pair_recv.at[f, 0], device_id={"seq": peer(1)}),
            pltpu.make_async_remote_copy(
                src_ref=pair.at[f, 1 - core], dst_ref=gotpair.at[f], send_sem=pair_send.at[f, 1],
                recv_sem=pair_recv.at[f, 1], device_id={"seq": peer(1)}),
        ]

    def transfer(f, other, slot):
        return [
            pltpu.make_async_remote_copy(
                src_ref=stat.at[f, other // 2], dst_ref=gotstat.at[f, slot], send_sem=stat_send.at[f, other // 2],
                recv_sem=stat_recv.at[f, slot], device_id={"seq": other}),
            pltpu.make_async_remote_copy(
                src_ref=send.at[f, other // 2], dst_ref=got.at[f, slot], send_sem=send_sem.at[f, other // 2],
                recv_sem=recv_sem.at[f, slot], device_id={"seq": other}),
        ]

    def messages(f):
        out = []
        for step in range(num_dev - 2, 0, -2):
            out += transfer(f, peer(step), mine)
        return out

    def arrivals(f):
        out = []
        for step in range(num_dev - 2, 0, -2):
            out += transfer(f, peer(step), peer(step) // 2)
        return out

    for f in range(frames):
        planes[f].wait()
        block = xbuf[f]
        full = jnp.dot(stack, block, preferred_element_type=F32)
        values = block.astype(F32)
        mean = jnp.sum(values, axis=0, keepdims=True) * (1.0 / feat)
        centred = values - mean
        spread = jnp.sum(centred * centred, axis=0, keepdims=True)
        part = full[:patch] + full[patch:] - sums * mean
        flat = jnp.transpose(part).reshape(pairs, 2, 2, half, patch)
        for c in range(2):
            pair[f, c] = jnp.concatenate([flat[:, c, 0], flat[:, c, 1]], axis=-1)
            for i in range(pairs):
                at = slice((2 * i + c) * tile, (2 * i + c + 1) * tile)
                pairstat[f, c, i, 0:1, 0:tile] = mean[:, at]
                pairstat[f, c, i, 1:2, 0:tile] = spread[:, at]
                pairstat[f, c, i, 2:3, :] = line[0:1]
                pairstat[f, c, i, 3:8, :] = jnp.zeros((5, 128), F32)
        if f == 0:
            pl.semaphore_wait(barrier, num_dev - 1)
        for copy in swap(f):
            copy.start()
    for f in range(frames):
        for copy in swap(f):
            copy.wait_recv()
        send[f] = (pair[f, core] + gotpair[f]).astype(BF16)
        stat[f, :, 0:3, :] = pairstat[f, core, :, 0:3, :]
        stat[f, :, 3:6, :] = gotpairstat[f, :, 0:3, :]
        for copy in messages(f):
            copy.start()
        got[f, mine] = send[f, mine]
        gotstat[f, mine] = stat[f, mine]

    for copy in weights:
        copy.wait()
    taps = [[jnp.transpose(upbuf[r, c].astype(F32)) for c in range(3)] for r in range(3)]
    for p in range(2):
        for i in range(2):
            group = ((0,), (1, 2)) if p == 0 else ((0, 1), (2,))
            tall = [functools.reduce(lambda a, b: a + b, [taps[r][c] for r in group[i]]) for c in range(3)]
            for q in range(2):
                first = tall[0] if q == 0 else tall[0] + tall[1]
                second = tall[1] + tall[2] if q == 0 else tall[2]
                w2_ref[p, i, q, 0:c1, :] = first.astype(BF16)
                w2_ref[p, i, q, c1 : 2 * c1, :] = second.astype(BF16)
    w3_ref[...] = jnp.zeros(w3_ref.shape, BF16)
    b1_ref[...] = b1buf[...].reshape(1, c1)
    g1_ref[...] = g1buf[...].reshape(1, c1)
    b2_ref[...] = b2buf[...].reshape(1, c2)
    g2_ref[...] = g2buf[...].reshape(1, c2)
    b3 = jnp.concatenate([b3buf[...].reshape(1, c3), jnp.zeros((1, 128 - c3), F32)], axis=1)
    ch = patch // 4
    blank = jnp.zeros((ch, c1), BF16)
    for a in range(2):
        for b in range(3):
            for j in range(4):
                spot = slice((4 * b + j) * ch, (4 * b + j + 1) * ch)
                w1s[a, spot, 0:c1] = w1buf[a + 1, b, j] if j < 3 else blank
                w1s[a, spot, c1 : 2 * c1] = w1buf[a + 1, b, j - 1] if j > 0 else blank
    for b in range(3):
        for e in range(3):
            w3_ref[b, e * 256 : e * 256 + c2, 0:c3] = outbuf[1, b, e]
            w3_ref[b, e * 256 : e * 256 + c2, 128 : 128 + c3] = outbuf[0, b, e]

    def to_next(f):
        return pltpu.make_async_remote_copy(
            src_ref=rows.at[f, 1], dst_ref=rows.at[f, 0], send_sem=halo_send.at[f, 0],
            recv_sem=halo_recv.at[f, 0], device_id={"seq": lax.rem(me + 1, num_dev)})

    def to_last(f):
        return pltpu.make_async_remote_copy(
            src_ref=rows.at[f, 1], dst_ref=rows.at[f, 2], send_sem=halo_send.at[f, 1],
            recv_sem=halo_recv.at[f, 1], device_id={"seq": lax.rem(me + num_dev - 1, num_dev)})

    def merge(f):
        for copy in arrivals(f):
            copy.wait_recv()
        means = jnp.concatenate([gotstat[f, :, 0, :], gotstat[f, :, 3, :]], axis=0)
        off = means - jnp.mean(means, axis=0, keepdims=True)
        spread = jnp.sum(gotstat[f, :, 1, :] + gotstat[f, :, 4, :], axis=0, keepdims=True)
        var = (spread + feat * jnp.sum(off * off, axis=0, keepdims=True)) * (1.0 / width)
        scale = jnp.transpose(jnp.broadcast_to(lax.rsqrt(var + 1e-06), (8, 128)))[0:tile, 0:1]
        lines = jnp.concatenate([gotstat[f, :, 2, :], gotstat[f, :, 5, :]], axis=0)
        fixed = jnp.dot(jnp.transpose(off), lines[:, 0:patch], precision=HIGH, preferred_element_type=F32)[0:tile]
        total_base = jnp.sum(lines, axis=0, keepdims=True)[:, patch:] + biasbuf[...].reshape(1, patch)
        summed = got[f, 0].astype(F32)
        for i in range(1, pairs):
            summed = summed + got[f, i].astype(F32)
        summed = jnp.concatenate([summed[:, :patch], summed[:, patch:]], axis=0)
        done = ((summed + fixed) * scale + total_base).astype(BF16).astype(F32)
        rows[f, 1] = jnp.concatenate([done[:half], done[half:]], axis=1).astype(BF16)

        @pl.when(me < num_dev - 1)
        def _():
            to_next(f).start()

        @pl.when(me > 0)
        def _():
            to_last(f).start()

        @pl.when(me == 0)
        def _():
            rows[f, 0] = jnp.zeros((half, 128), BF16)

        @pl.when(me == num_dev - 1)
        def _():
            rows[f, 2] = jnp.zeros((half, 128), BF16)

    def gather(f):
        @pl.when(me > 0)
        def _():
            to_next(f).wait_recv()

        @pl.when(me < num_dev - 1)
        def _():
            to_last(f).wait_recv()

        quads = []
        col = lax.broadcasted_iota(jnp.int32, (tile, 1), 0)
        for h in range(3):
            pair = rows[f, h].astype(F32)
            token = jnp.concatenate([pair[:, :patch], pair[:, patch:]], axis=0)
            before = jnp.where(col == 0, 0.0, pltpu.roll(token, 1, 0))
            after = jnp.where(col == tile - 1, 0.0, pltpu.roll(token, tile - 1, 0))
            for q in range(2):
                a = 2 * q * ch
                quads.append(jnp.concatenate(
                    [before[:, a + ch : a + 2 * ch], token[:, a : a + 2 * ch], after[:, a : a + ch]], axis=1))
        for i in range(4):
            x1_ref[f, i] = jnp.concatenate(quads[i : i + 3], axis=1).astype(BF16)

    merge(0)
    gather(0)
    stage_in(num_dev, me, 0, x1_ref, w1s, b1_ref, g1_ref, act1)
    stage_up(num_dev, me, act1, w2_ref, b2_ref, g2_ref, act2)
    merge(1)
    m3 = (act2.shape[0] - 2) * TOK_W
    for s in range(4):
        old = stage_out(act2, w3_ref, slice(0, 256), s)
        res_ref[pl.ds(s, m3, stride=4), :] = old[:, 0:128] + b3
        res_ref[pl.ds(4 * m3 + s, m3, stride=4), :] = old[:, 128:256] + b3
    gather(1)

    for f in range(frames):
        for copy in swap(f) + messages(f):
            copy.wait_send()
        @pl.when(me < num_dev - 1)
        def _():
            to_next(f).wait_send()

        @pl.when(me > 0)
        def _():
            to_last(f).wait_send()


def local(
    hidden, mod_shift, mod_scale, head_weight, head_bias, conv_in_weight, conv_in_bias, gain_in,
    up_weight, up_bias, gain_up, out_weight, out_bias,
):
    num_dev = lax.axis_size("seq")
    frames, feat, tok_total = hidden.shape
    tile = tok_total // num_dev
    rows_dev = tile // TOK_W
    patch, width = head_weight.shape
    lat_ch, c1 = conv_in_weight.shape[3:]
    c2, c3 = out_weight.shape[3:]
    lat_rows = 2 * rows_dev
    window = min(width, (feat + 255 - math.gcd(feat, 128)) // 128 * 128)
    vmem = pl.BlockSpec(memory_space=pltpu.VMEM)
    hbm = pl.BlockSpec(memory_space=pltpu.HBM)
    half = tile // 2
    pairs = num_dev // 2
    raw = (hidden, head_weight, mod_scale[None], mod_shift[None], head_bias,
           jnp.transpose(up_weight, (0, 1, 3, 2)), out_weight, conv_in_weight,
           conv_in_bias, gain_in, up_bias, gain_up, out_bias)
    cells = frames * 2 * lat_rows * 4 * TOK_W
    act1 = pltpu.VMEM((lat_rows + 2, TOK_W, 4 * c1), BF16)
    act2 = pltpu.VMEM((2 * lat_rows + 2, TOK_W, 6 * 256), BF16)
    made = pl.pallas_call(
        functools.partial(exchange_kernel, num_dev),
        out_shape=[
            jax.ShapeDtypeStruct((frames, lat_rows + 2, TOK_W, 12 * lat_ch), BF16),
            jax.ShapeDtypeStruct((2, 12 * lat_ch, 2 * c1), BF16),
            jax.ShapeDtypeStruct((2, 2, 2, 2 * c1, c2), BF16),
            jax.ShapeDtypeStruct((3, 768, 256), BF16),
            jax.ShapeDtypeStruct((1, c1), F32),
            jax.ShapeDtypeStruct((1, c1), F32),
            jax.ShapeDtypeStruct((1, c2), F32),
            jax.ShapeDtypeStruct((1, c2), F32),
            jax.ShapeDtypeStruct((cells, 128), F32),
        ],
        in_specs=[hbm] * len(raw),
        out_specs=[vmem] * 9,
        scratch_shapes=[
            pltpu.VMEM((frames, feat, tok_total), BF16),
            pltpu.VMEM((patch, window), F32),
            pltpu.VMEM((2, 1, window), F32),
            pltpu.VMEM((3, 3, c2, c1), BF16),
            pltpu.VMEM((2, 3, 3, c2, c3), BF16),
            pltpu.VMEM((3, 3, 3, lat_ch, c1), BF16),
            pltpu.VMEM((patch,), F32),
            pltpu.VMEM((c1,), F32),
            pltpu.VMEM((c1,), F32),
            pltpu.VMEM((c2,), F32),
            pltpu.VMEM((c2,), F32),
            pltpu.VMEM((c3,), F32),
            act1,
            act2,
            pltpu.VMEM((frames, 2, pairs, half, 2 * patch), F32),
            pltpu.VMEM((frames, 2, pairs, 8, 128), F32),
            pltpu.VMEM((frames, pairs, half, 2 * patch), F32),
            pltpu.VMEM((frames, pairs, 8, 128), F32),
            pltpu.VMEM((frames, pairs, half, 2 * patch), BF16),
            pltpu.VMEM((frames, pairs, 8, 128), F32),
            pltpu.VMEM((frames, pairs, half, 2 * patch), BF16),
            pltpu.VMEM((frames, pairs, 8, 128), F32),
            pltpu.VMEM((frames, 3, half, 2 * patch), BF16),
            pltpu.SemaphoreType.DMA((5,)),
            pltpu.SemaphoreType.DMA((9,)),
            pltpu.SemaphoreType.DMA((frames, 2)),
            pltpu.SemaphoreType.DMA((frames, 2)),
            pltpu.SemaphoreType.DMA((frames, pairs)),
            pltpu.SemaphoreType.DMA((frames, pairs)),
            pltpu.SemaphoreType.DMA((frames, pairs)),
            pltpu.SemaphoreType.DMA((frames, pairs)),
            pltpu.SemaphoreType.DMA((frames, 2)),
            pltpu.SemaphoreType.DMA((frames, 2)),
        ],
        compiler_params=pltpu.CompilerParams(
            vmem_limit_bytes=26 * 1024 * 1024, collective_id=0, has_side_effects=True),
    )(*[pltpu.with_memory_space_constraint(value, pltpu.HBM) for value in raw])
    x1, w1s, w2, w3, b1, g1, b2, g2, res = made
    out = pl.pallas_call(
        functools.partial(conv_kernel, num_dev),
        out_shape=jax.ShapeDtypeStruct((frames * 2 * lat_rows, c3, 4 * TOK_W), BF16),
        in_specs=[vmem] * 9,
        out_specs=hbm,
        scratch_shapes=[
            act1,
            act2,
            pltpu.VMEM((cells // 2, 128), F32),
            pltpu.VMEM((frames * 2 * lat_rows, c3, 4 * TOK_W), BF16),
            pltpu.SemaphoreType.DMA((frames * 2 * lat_rows,)),
        ],
        compiler_params=pltpu.CompilerParams(vmem_limit_bytes=26 * 1024 * 1024),
    )(x1, w1s, b1, g1, w2, b2, g2, w3, res)
    return out.reshape(frames, 2 * lat_rows, c3, 4 * TOK_W).transpose(0, 1, 3, 2)


def solution(mesh):
    placed = (P("grp", "seq", None), P(), P(), P(), P(), P(), P(), P(), P(), P(), P(), P(), P())
    return jax.shard_map(
        local, mesh=mesh, in_specs=placed, out_specs=P("grp", "seq", None, None), check_vma=False
    )
```

time: 31.5 us -> 27.2 us (0.86)
  Pallas kernels: 31.3 us -> 26.9 us
    pallas_call x1, Pallas kernels: 9.28 us -> 5.47 us  [local(): pl.pallas_call(functools.partial(conv_kernel, num_dev), out_shape=jax.Sha...]
    pallas_call x1, Pallas kernels: 22 us -> 21.4 us  [local(): pl.pallas_call(functools.partial(exchange_kernel, num_dev), out_shape=[ja...]
where the time goes in v2:
time: 27.2 us; the launch traced here: 27.1 us
  Pallas kernels  26.9 us (99%)
    pallas_call x1, Pallas kernels, local(): pl.pallas_call(functools.partial(exchange_kernel, num_dev), out_shape=[ja...  21.4 us
    pallas_call x1, Pallas kernels, local(): pl.pallas_call(functools.partial(conv_kernel, num_dev), out_shape=jax.Sha...  5.47 us

profile of v2, /device:TPU:1, one launch (start us, length us, event | category | flops | bytes accessed | tf_op | source)
XLA Modules:
  0.0 27.1 jit_solution(1005959841032380996)
XLA Ops:
  0.0 21.4 %shard_map.127 = (bf16[2,4,80,192]{3,2,1,0:T(8,128)(2,1)S(1)}, bf16[2,192,768]{2,1,0:T(8,128)(2,1)S(1)}, bf16[2,2,2,768,192]{4,3,2,1,0:T(8,128)(2,1)S(1)}, bf16[...) custom-call(bf16[2,320,1280]{2,1,0:T(8,128)(2,1)} %x_hbm.1, ...), custom_call_target="tpu_custom_call" | custom-call | tf_op jit(solution)/shard_map/pallas_call | solution.py:399
  21.4 5.5 %shard_map.128 = bf16[8,96,320]{2,1,0:T(8,128)(2,1)} custom-call(bf16[2,4,80,192]{3,2,1,0:T(8,128)(2,1)S(1)} %get-tuple-element.14.x_ref, bf16[2,192,768]{2,1,0:T(8,128)(2,1)S(1)} %get-tuple-element.15.w1s, f32[1,384]{1,0:T(1,128)S(1)} %get-tuple-element.16.b1_ref, f32[1,384]{1,0:T(1,128)S(1)} %get-tuple-element.17.g1_ref, ...), custom_call_target="tpu_custom_call" | custom-call | tf_op jit(solution)/shard_map/pallas_call | solution.py:453

commit v3 on v2

--- a/solution.py
+++ b/solution.py
@@ -84,13 +84,13 @@
                     act2[2 * i + 1 - p, :, spot * 256 : (spot + 1) * 256] = piece[i]
 
 
-def stage_out(act2, w3_ref, part, s):
+def stage_out(act2, weight, s, cols):
     rows3 = act2.shape[0] - 2
-    lanes = slice(s * 256, (s + 3) * 256)
+    lanes = slice(s * 256, (s + cols) * 256)
     total = None
     for b in range(3):
-        block = act2[b : b + rows3, :, lanes].reshape(rows3 * TOK_W, 768)
-        one = jnp.dot(block, w3_ref[b, :, part], preferred_element_type=F32)
+        block = act2[b : b + rows3, :, lanes].reshape(rows3 * TOK_W, cols * 256)
+        one = jnp.dot(block, weight[b], preferred_element_type=F32)
         total = one if total is None else total + one
     return total
 
@@ -108,9 +108,11 @@
         obuf[i] = jnp.transpose(res_ref[i * width : (i + 1) * width, :])[0:c3].astype(BF16)
         copies[i].start()
     stage_up(num_dev, dev, act1, w2_ref, b2_ref, g2_ref, act2)
-    for s in range(4):
-        new = stage_out(act2, w3_ref, slice(0, 128), s)
-        res[pl.ds(s, m3, stride=4), :] = new + res_ref[pl.ds(4 * m3 + s, m3, stride=4), :]
+    for s in (0, 2):
+        new = stage_out(act2, w3_ref, s, 4)
+        for g in range(2):
+            old = res_ref[pl.ds(4 * m3 + s + g, m3, stride=4), :]
+            res[pl.ds(s + g, m3, stride=4), :] = new[:, g * 128 : (g + 1) * 128] + old
     for i in range(rows3):
         obuf[rows3 + i] = jnp.transpose(res[i * width : (i + 1) * width, :])[0:c3].astype(BF16)
         copies[rows3 + i].start()
@@ -121,7 +123,7 @@
 def exchange_kernel(num_dev, x_hbm, w_hbm, scale_hbm, shift_hbm, bias_hbm, up_hbm, outw_hbm, w1_hbm,
                     b1_hbm, g1_hbm, b2_hbm, g2_hbm, b3_hbm,
                     x1_ref, w1s, w2_ref, w3_ref, b1_ref, g1_ref, b2_ref, g2_ref, res_ref,
-                    xbuf, wbuf, modbuf, upbuf, outbuf, w1buf, biasbuf, b1buf, g1buf, b2buf, g2buf, b3buf, act1, act2, pair, pairstat, gotpair, gotpairstat, send, stat, got, gotstat, rows,
+                    xbuf, wbuf, modbuf, upbuf, outbuf, w1buf, biasbuf, b1buf, g1buf, b2buf, g2buf, b3buf, w3s, act1, act2, pair, pairstat, gotpair, gotpairstat, send, stat, got, gotstat, rows,
                     in_sem, weight_sem, pair_send, pair_recv, send_sem, recv_sem, stat_send, stat_recv, halo_send, halo_recv):
     frames, feat, total = x_hbm.shape
     patch, width = w_hbm.shape
@@ -263,6 +265,7 @@
                 second = tall[1] + tall[2] if q == 0 else tall[2]
                 w2_ref[p, i, q, 0:c1, :] = first.astype(BF16)
                 w2_ref[p, i, q, c1 : 2 * c1, :] = second.astype(BF16)
+    w3s[...] = jnp.zeros(w3s.shape, BF16)
     w3_ref[...] = jnp.zeros(w3_ref.shape, BF16)
     b1_ref[...] = b1buf[...].reshape(1, c1)
     g1_ref[...] = g1buf[...].reshape(1, c1)
@@ -279,8 +282,10 @@
                 w1s[a, spot, c1 : 2 * c1] = w1buf[a + 1, b, j - 1] if j > 0 else blank
     for b in range(3):
         for e in range(3):
-            w3_ref[b, e * 256 : e * 256 + c2, 0:c3] = outbuf[1, b, e]
-            w3_ref[b, e * 256 : e * 256 + c2, 128 : 128 + c3] = outbuf[0, b, e]
+            w3s[b, e * 256 : e * 256 + c2, 0:c3] = outbuf[1, b, e]
+            w3s[b, e * 256 : e * 256 + c2, 128 : 128 + c3] = outbuf[0, b, e]
+            for g in range(2):
+                w3_ref[b, (e + g) * 256 : (e + g) * 256 + c2, g * 128 : g * 128 + c3] = outbuf[1, b, e]
 
     def to_next(f):
         return pltpu.make_async_remote_copy(
@@ -356,7 +361,7 @@
     merge(1)
     m3 = (act2.shape[0] - 2) * TOK_W
     for s in range(4):
-        old = stage_out(act2, w3_ref, slice(0, 256), s)
+        old = stage_out(act2, w3s, s, 3)
         res_ref[pl.ds(s, m3, stride=4), :] = old[:, 0:128] + b3
         res_ref[pl.ds(4 * m3 + s, m3, stride=4), :] = old[:, 128:256] + b3
     gather(1)
@@ -402,7 +407,7 @@
             jax.ShapeDtypeStruct((frames, lat_rows + 2, TOK_W, 12 * lat_ch), BF16),
             jax.ShapeDtypeStruct((2, 12 * lat_ch, 2 * c1), BF16),
             jax.ShapeDtypeStruct((2, 2, 2, 2 * c1, c2), BF16),
-            jax.ShapeDtypeStruct((3, 768, 256), BF16),
+            jax.ShapeDtypeStruct((3, 1024, 256), BF16),
             jax.ShapeDtypeStruct((1, c1), F32),
             jax.ShapeDtypeStruct((1, c1), F32),
             jax.ShapeDtypeStruct((1, c2), F32),
@@ -424,6 +429,7 @@
             pltpu.VMEM((c2,), F32),
             pltpu.VMEM((c2,), F32),
             pltpu.VMEM((c3,), F32),
+            pltpu.VMEM((3, 768, 256), BF16),
             act1,
             act2,
             pltpu.VMEM((frames, 2, pairs, half, 2 * patch), F32),

time: 27.2 us -> 26.2 us (0.963)
  Pallas kernels: 26.9 us -> 26.1 us
    pallas_call x1, Pallas kernels: 5.47 us -> 4.79 us  [local(): pl.pallas_call(functools.partial(conv_kernel, num_dev), out_shape=jax.Sha...]
where the time goes in v3:
time: 26.2 us; the launch traced here: 26.1 us
  Pallas kernels  26.1 us (100%)
    pallas_call x1, Pallas kernels, local(): pl.pallas_call(functools.partial(exchange_kernel, num_dev), out_shape=[ja...  21.3 us
    pallas_call x1, Pallas kernels, local(): pl.pallas_call(functools.partial(conv_kernel, num_dev), out_shape=jax.Sha...  4.79 us

profile of v3, /device:TPU:1, one launch (start us, length us, event | category | flops | bytes accessed | tf_op | source)
XLA Modules:
  0.0 26.1 jit_solution(1207581678822961203)
XLA Ops:
  0.0 21.3 %shard_map.127 = (bf16[2,4,80,192]{3,2,1,0:T(8,128)(2,1)S(1)}, bf16[2,192,768]{2,1,0:T(8,128)(2,1)S(1)}, bf16[2,2,2,768,192]{4,3,2,1,0:T(8,128)(2,1)S(1)}, bf16[...) custom-call(bf16[2,320,1280]{2,1,0:T(8,128)(2,1)} %x_hbm.1, ...), custom_call_target="tpu_custom_call" | custom-call | tf_op jit(solution)/shard_map/pallas_call | solution.py:404
  21.3 4.8 %shard_map.128 = bf16[8,96,320]{2,1,0:T(8,128)(2,1)} custom-call(bf16[2,4,80,192]{3,2,1,0:T(8,128)(2,1)S(1)} %get-tuple-element.14.x_ref, bf16[2,192,768]{2,1,0:T(8,128)(2,1)S(1)} %get-tuple-element.15.w1s, f32[1,384]{1,0:T(1,128)S(1)} %get-tuple-element.16.b1_ref, f32[1,384]{1,0:T(1,128)S(1)} %get-tuple-element.17.g1_ref, ...), custom_call_target="tpu_custom_call" | custom-call | tf_op jit(solution)/shard_map/pallas_call | solution.py:459

commit v4 on v3

--- a/solution.py
+++ b/solution.py
@@ -33,7 +33,7 @@
     return (row >= 0) & (row < total)
 
 
-def stage_in(num_dev, dev, frame, x_ref, w1s, b1_ref, g1_ref, act1):
+def stage_in(num_dev, dev, frame, x_ref, w1s, b1_ref, g1_ref, act1, edge1):
     rows1 = x_ref.shape[1]
     lat_rows = rows1 - 2
     c1 = g1_ref.shape[1]
@@ -47,69 +47,97 @@
     for r in range(2):
         val = rms_silu(pre[:, r * c1 : (r + 1) * c1] + b1_ref[...], g1_ref[...])
         val = jnp.where(keep1, val, 0.0)
-        edge = shift_cols(val, 1) if r == 1 else shift_cols(val, -1)
-        spot = 0 if r == 1 else 3
-        act1[:, :, (r + 1) * c1 : (r + 2) * c1] = val.astype(BF16).reshape(rows1, TOK_W, c1)
-        act1[:, :, spot * c1 : (spot + 1) * c1] = edge.astype(BF16).reshape(rows1, TOK_W, c1)
-
-
-def stage_up(num_dev, dev, act1, w2_ref, b2_ref, g2_ref, act2):
+        act1[:, :, r * c1 : (r + 1) * c1] = val.astype(BF16).reshape(rows1, TOK_W, c1)
+        if r == 0:
+            moved = shift_cols(val, -1)
+            act1[:, :, 2 * c1 : 3 * c1] = moved.astype(BF16).reshape(rows1, TOK_W, c1)
+            firsts = [val[i * TOK_W : i * TOK_W + 1] for i in range(rows1)]
+            fill = [jnp.zeros((17 - rows1, c1), F32)]
+            for k in range(2):
+                edge1[k, :, 0:c1] = jnp.zeros((16, c1), BF16)
+                edge1[k, :, c1 : 2 * c1] = jnp.concatenate(firsts[k : k + rows1 - 1] + fill, axis=0).astype(BF16)
+
+
+def silu(values):
+    return values * jax.nn.sigmoid(values)
+
+
+def stage_up(num_dev, dev, act1, edge1, w2_ref, b2_ref, g2_ref, chans, act2):
     rows2 = act1.shape[0] - 1
     lat_rows = rows2 - 1
-    c1 = act1.shape[2] // 4
-    c2 = g2_ref.shape[1]
+    c1 = act1.shape[2] // 3
     m2 = rows2 * TOK_W
-    start = (0, 1, 1, 2)
-    for p in range(2):
-        first = 0 if p == 0 else -1
-        keep2 = inside(m2, 2 * dev * lat_rows + first, 2, 2 * num_dev * lat_rows)
-        for s in range(4):
-            q = s % 2
-            lanes = slice(start[s] * c1, (start[s] + 2) * c1)
-            top = act1[0:rows2, :, lanes].reshape(m2, 2 * c1)
-            low = act1[1 : rows2 + 1, :, lanes].reshape(m2, 2 * c1)
-            pre = jnp.dot(top, w2_ref[p, 0, q], preferred_element_type=F32)
-            pre = pre + jnp.dot(low, w2_ref[p, 1, q], preferred_element_type=F32)
-            val = rms_silu(pre + b2_ref[...], g2_ref[...])
-            val = jnp.where(keep2, val, 0.0)
-            val = jnp.concatenate([val, jnp.zeros((m2, 256 - c2), F32)], axis=1)
-            pieces = [(s + 1, val)]
-            if s == 3:
-                pieces.append((0, shift_cols(val, 1)))
-            if s == 0:
-                pieces.append((5, shift_cols(val, -1)))
-            for spot, piece in pieces:
-                piece = piece.astype(BF16).reshape(rows2, TOK_W, 256)
+    left = lax.broadcasted_iota(jnp.int32, (1, 128), 1) < chans - 128
+    for t in range(2):
+        lanes = slice(t * c1, (t + 2) * c1)
+        top = act1[0:rows2, :, lanes].reshape(m2, 2 * c1)
+        low = act1[1 : rows2 + 1, :, lanes].reshape(m2, 2 * c1)
+        if t == 1:
+            top = jnp.concatenate([top, edge1[0]], axis=0)
+            low = jnp.concatenate([low, edge1[1]], axis=0)
+        count = top.shape[0]
+        pre = jnp.dot(top, w2_ref[0], preferred_element_type=F32)
+        pre = pre + jnp.dot(low, w2_ref[1], preferred_element_type=F32)
+        index = lax.broadcasted_iota(jnp.int32, (count, 1), 0)
+        row = jnp.where(index < m2, index // TOK_W, index - m2)
+        for p in range(2):
+            a = pre[:, p * 384 : p * 384 + 128] + b2_ref[:, 0:128]
+            b = pre[:, p * 384 + 128 : p * 384 + 256] + b2_ref[:, 0:128]
+            h = pre[:, p * 384 + 256 : p * 384 + 384] + b2_ref[:, 128:256]
+            sq = h * h
+            sum_a = jnp.sum(a * a + jnp.where(left, sq, 0.0), axis=-1, keepdims=True)
+            sum_b = jnp.sum(b * b + jnp.where(left, 0.0, sq), axis=-1, keepdims=True)
+            inv_a = lax.rsqrt(sum_a * (1.0 / chans) + 1e-06)
+            inv_b = lax.rsqrt(sum_b * (1.0 / chans) + 1e-06)
+            line = 2 * dev * lat_rows + 2 * row - p
+            keep = (line >= 0) & (line < 2 * num_dev * lat_rows)
+            keep_a, keep_b = keep, keep
+            if t == 1:
+                keep_a = keep & (index < m2)
+                keep_b = keep & ((index >= m2) | (index % TOK_W != TOK_W - 1))
+            gain_a = jnp.where(keep_a, inv_a, 0.0)
+            gain_b = jnp.where(keep_b, inv_b, 0.0)
+            a = silu(a * gain_a * g2_ref[:, 0:128])
+            b = silu(b * gain_b * g2_ref[:, 0:128])
+            h = silu(h * jnp.where(left, gain_a, gain_b) * g2_ref[:, 128:256])
+            val = jnp.concatenate([a, b, h], axis=1)
+            main = val[0:m2]
+            piece = main.astype(BF16).reshape(rows2, TOK_W, 384)
+            for i in range(rows2):
+                act2[2 * i + 1 - p, :, (t + 1) * 384 : (t + 2) * 384] = piece[i]
+            if t == 1:
+                moved = pltpu.roll(main, 1, 0)
+                col = lax.broadcasted_iota(jnp.int32, (TOK_W, 1), 0)
                 for i in range(rows2):
-                    act2[2 * i + 1 - p, :, spot * 256 : (spot + 1) * 256] = piece[i]
-
-
-def stage_out(act2, weight, s, cols):
+                    block = jnp.where(col == 0, val[m2 + i : m2 + i + 1], moved[i * TOK_W : (i + 1) * TOK_W])
+                    act2[2 * i + 1 - p, :, 0:384] = block.astype(BF16)
+
+
+def stage_out(act2, w3_ref, part, t):
     rows3 = act2.shape[0] - 2
-    lanes = slice(s * 256, (s + cols) * 256)
     total = None
     for b in range(3):
-        block = act2[b : b + rows3, :, lanes].reshape(rows3 * TOK_W, cols * 256)
-        one = jnp.dot(block, weight[b], preferred_element_type=F32)
+        block = act2[b : b + rows3, :, t * 384 : t * 384 + 768].reshape(rows3 * TOK_W, 768)
+        one = jnp.dot(block, w3_ref[part, b], preferred_element_type=F32)
         total = one if total is None else total + one
     return total
 
 
-def conv_kernel(num_dev, x_ref, w1s, b1_ref, g1_ref, w2_ref, b2_ref, g2_ref, w3_ref, res_ref, out_hbm,
-                act1, act2, res, obuf, out_sem):
+def conv_kernel(num_dev, chans, x_ref, w1s, b1_ref, g1_ref, w2_ref, b2_ref, g2_ref, w3_ref, res_ref, out_hbm,
+                act1, edge1, act2, res, obuf, out_sem):
     dev = lax.axis_index("seq")
     rows3 = act2.shape[0] - 2
     m3 = rows3 * TOK_W
     c3 = obuf.shape[1]
     width = 4 * TOK_W
     copies = [pltpu.make_async_copy(obuf.at[i], out_hbm.at[i], out_sem.at[i]) for i in range(2 * rows3)]
-    stage_in(num_dev, dev, 1, x_ref, w1s, b1_ref, g1_ref, act1)
+    stage_in(num_dev, dev, 1, x_ref, w1s, b1_ref, g1_ref, act1, edge1)
     for i in range(rows3):
         obuf[i] = jnp.transpose(res_ref[i * width : (i + 1) * width, :])[0:c3].astype(BF16)
         copies[i].start()
-    stage_up(num_dev, dev, act1, w2_ref, b2_ref, g2_ref, act2)
+    stage_up(num_dev, dev, act1, edge1, w2_ref, b2_ref, g2_ref, chans, act2)
     for s in (0, 2):
-        new = stage_out(act2, w3_ref, s, 4)
+        new = stage_out(act2, w3_ref, 0, s // 2)
         for g in range(2):
             old = res_ref[pl.ds(4 * m3 + s + g, m3, stride=4), :]
             res[pl.ds(s + g, m3, stride=4), :] = new[:, g * 128 : (g + 1) * 128] + old
@@ -123,7 +151,7 @@
 def exchange_kernel(num_dev, x_hbm, w_hbm, scale_hbm, shift_hbm, bias_hbm, up_hbm, outw_hbm, w1_hbm,
                     b1_hbm, g1_hbm, b2_hbm, g2_hbm, b3_hbm,
                     x1_ref, w1s, w2_ref, w3_ref, b1_ref, g1_ref, b2_ref, g2_ref, res_ref,
-                    xbuf, wbuf, modbuf, upbuf, outbuf, w1buf, biasbuf, b1buf, g1buf, b2buf, g2buf, b3buf, w3s, act1, act2, pair, pairstat, gotpair, gotpairstat, send, stat, got, gotstat, rows,
+                    xbuf, wbuf, modbuf, upbuf, outbuf, w1buf, biasbuf, b1buf, g1buf, b2buf, g2buf, b3buf, act1, edge1, act2, pair, pairstat, gotpair, gotpairstat, send, stat, got, gotstat, rows,
                     in_sem, weight_sem, pair_send, pair_recv, send_sem, recv_sem, stat_send, stat_recv, halo_send, halo_recv):
     frames, feat, total = x_hbm.shape
     patch, width = w_hbm.shape
@@ -263,14 +291,19 @@
             for q in range(2):
                 first = tall[0] if q == 0 else tall[0] + tall[1]
                 second = tall[1] + tall[2] if q == 0 else tall[2]
-                w2_ref[p, i, q, 0:c1, :] = first.astype(BF16)
-                w2_ref[p, i, q, c1 : 2 * c1, :] = second.astype(BF16)
-    w3s[...] = jnp.zeros(w3s.shape, BF16)
+                for k, half_w in enumerate((first, second)):
+                    down = slice(k * c1, (k + 1) * c1)
+                    lo = p * 384 + (1 - q) * 128
+                    hi = p * 384 + 256 + (1 - q) * (c2 - 128)
+                    w2_ref[i, down, lo : lo + 128] = half_w[:, 0:128].astype(BF16)
+                    w2_ref[i, down, hi : hi + c2 - 128] = half_w[:, 128:c2].astype(BF16)
     w3_ref[...] = jnp.zeros(w3_ref.shape, BF16)
     b1_ref[...] = b1buf[...].reshape(1, c1)
     g1_ref[...] = g1buf[...].reshape(1, c1)
-    b2_ref[...] = b2buf[...].reshape(1, c2)
-    g2_ref[...] = g2buf[...].reshape(1, c2)
+    b2 = b2buf[...].reshape(1, c2)
+    g2 = g2buf[...].reshape(1, c2)
+    b2_ref[...] = jnp.concatenate([b2, b2[:, 128:c2]], axis=1)
+    g2_ref[...] = jnp.concatenate([g2, g2[:, 128:c2]], axis=1)
     b3 = jnp.concatenate([b3buf[...].reshape(1, c3), jnp.zeros((1, 128 - c3), F32)], axis=1)
     ch = patch // 4
     blank = jnp.zeros((ch, c1), BF16)
@@ -282,10 +315,13 @@
                 w1s[a, spot, c1 : 2 * c1] = w1buf[a + 1, b, j - 1] if j > 0 else blank
     for b in range(3):
         for e in range(3):
-            w3s[b, e * 256 : e * 256 + c2, 0:c3] = outbuf[1, b, e]
-            w3s[b, e * 256 : e * 256 + c2, 128 : 128 + c3] = outbuf[0, b, e]
-            for g in range(2):
-                w3_ref[b, (e + g) * 256 : (e + g) * 256 + c2, g * 128 : g * 128 + c3] = outbuf[1, b, e]
+            for a in range(2):
+                for g in range(2):
+                    k = e + g
+                    lo = k // 2 * 384 + k % 2 * 128
+                    hi = k // 2 * 384 + 256 + k % 2 * (c2 - 128)
+                    w3_ref[a, b, lo : lo + 128, g * 128 : g * 128 + c3] = outbuf[1 - a, b, e, 0:128, :]
+                    w3_ref[a, b, hi : hi + c2 - 128, g * 128 : g * 128 + c3] = outbuf[1 - a, b, e, 128:c2, :]
 
     def to_next(f):
         return pltpu.make_async_remote_copy(
@@ -356,14 +392,15 @@
 
     merge(0)
     gather(0)
-    stage_in(num_dev, me, 0, x1_ref, w1s, b1_ref, g1_ref, act1)
-    stage_up(num_dev, me, act1, w2_ref, b2_ref, g2_ref, act2)
+    stage_in(num_dev, me, 0, x1_ref, w1s, b1_ref, g1_ref, act1, edge1)
+    stage_up(num_dev, me, act1, edge1, w2_ref, b2_ref, g2_ref, c2, act2)
     merge(1)
     m3 = (act2.shape[0] - 2) * TOK_W
-    for s in range(4):
-        old = stage_out(act2, w3s, s, 3)
-        res_ref[pl.ds(s, m3, stride=4), :] = old[:, 0:128] + b3
-        res_ref[pl.ds(4 * m3 + s, m3, stride=4), :] = old[:, 128:256] + b3
+    for s in (0, 2):
+        for a in range(2):
+            old = stage_out(act2, w3_ref, a, s // 2)
+            for g in range(2):
+                res_ref[pl.ds(4 * m3 * a + s + g, m3, stride=4), :] = old[:, g * 128 : (g + 1) * 128] + b3
     gather(1)
 
     for f in range(frames):
@@ -399,19 +436,20 @@
            jnp.transpose(up_weight, (0, 1, 3, 2)), out_weight, conv_in_weight,
            conv_in_bias, gain_in, up_bias, gain_up, out_bias)
     cells = frames * 2 * lat_rows * 4 * TOK_W
-    act1 = pltpu.VMEM((lat_rows + 2, TOK_W, 4 * c1), BF16)
-    act2 = pltpu.VMEM((2 * lat_rows + 2, TOK_W, 6 * 256), BF16)
+    act1 = pltpu.VMEM((lat_rows + 2, TOK_W, 3 * c1), BF16)
+    edge1 = pltpu.VMEM((2, 16, 2 * c1), BF16)
+    act2 = pltpu.VMEM((2 * lat_rows + 2, TOK_W, 3 * 384), BF16)
     made = pl.pallas_call(
         functools.partial(exchange_kernel, num_dev),
         out_shape=[
             jax.ShapeDtypeStruct((frames, lat_rows + 2, TOK_W, 12 * lat_ch), BF16),
             jax.ShapeDtypeStruct((2, 12 * lat_ch, 2 * c1), BF16),
-            jax.ShapeDtypeStruct((2, 2, 2, 2 * c1, c2), BF16),
-            jax.ShapeDtypeStruct((3, 1024, 256), BF16),
+            jax.ShapeDtypeStruct((2, 2 * c1, 768), BF16),
+            jax.ShapeDtypeStruct((2, 3, 768, 256), BF16),
             jax.ShapeDtypeStruct((1, c1), F32),
             jax.ShapeDtypeStruct((1, c1), F32),
-            jax.ShapeDtypeStruct((1, c2), F32),
-            jax.ShapeDtypeStruct((1, c2), F32),
+            jax.ShapeDtypeStruct((1, 256), F32),
+            jax.ShapeDtypeStruct((1, 256), F32),
             jax.ShapeDtypeStruct((cells, 128), F32),
         ],
         in_specs=[hbm] * len(raw),
@@ -429,8 +467,8 @@
             pltpu.VMEM((c2,), F32),
             pltpu.VMEM((c2,), F32),
             pltpu.VMEM((c3,), F32),
-            pltpu.VMEM((3, 768, 256), BF16),
             act1,
+            edge1,
             act2,
             pltpu.VMEM((frames, 2, pairs, half, 2 * patch), F32),
             pltpu.VMEM((frames, 2, pairs, 8, 128), F32),
@@ -457,12 +495,13 @@
     )(*[pltpu.with_memory_space_constraint(value, pltpu.HBM) for value in raw])
     x1, w1s, w2, w3, b1, g1, b2, g2, res = made
     out = pl.pallas_call(
-        functools.partial(conv_kernel, num_dev),
+        functools.partial(conv_kernel, num_dev, c2),
         out_shape=jax.ShapeDtypeStruct((frames * 2 * lat_rows, c3, 4 * TOK_W), BF16),
         in_specs=[vmem] * 9,
         out_specs=hbm,
         scratch_shapes=[
             act1,
+            edge1,
             act2,
             pltpu.VMEM((cells // 2, 128), F32),
             pltpu.VMEM((frames * 2 * lat_rows, c3, 4 * TOK_W), BF16),

time: 26.2 us -> 25.1 us (0.958)
  Pallas kernels: 26.1 us -> 25 us
    pallas_call x1, Pallas kernels: 4.79 us -> 4.18 us  [local(): pl.pallas_call(functools.partial(conv_kernel, num_dev, c2), out_shape=jax...]
    pallas_call x1, Pallas kernels: 21.3 us -> 20.8 us  [local(): pl.pallas_call(functools.partial(exchange_kernel, num_dev), out_shape=[ja...]
where the time goes in v4:
time: 25.1 us; the launch traced here: 25 us
  Pallas kernels  25 us (100%)
    pallas_call x1, Pallas kernels, local(): pl.pallas_call(functools.partial(exchange_kernel, num_dev), out_shape=[ja...  20.8 us
    pallas_call x1, Pallas kernels, local(): pl.pallas_call(functools.partial(conv_kernel, num_dev, c2), out_shape=jax...  4.18 us

profile of v4, /device:TPU:1, one launch (start us, length us, event | category | flops | bytes accessed | tf_op | source)
XLA Modules:
  0.0 25.0 jit_solution(16646424052177997583)
XLA Ops:
  0.0 20.8 %shard_map.127 = (bf16[2,4,80,192]{3,2,1,0:T(8,128)(2,1)S(1)}, bf16[2,192,768]{2,1,0:T(8,128)(2,1)S(1)}, bf16[2,768,768]{2,1,0:T(8,128)(2,1)S(1)}, bf16[2,3,768,...) custom-call(bf16[2,320,1280]{2,1,0:T(8,128)(2,1)} %x_hbm.1, ...), custom_call_target="tpu_custom_call" | custom-call | tf_op jit(solution)/shard_map/pallas_call | solution.py:442
  20.8 4.2 %shard_map.128 = bf16[8,96,320]{2,1,0:T(8,128)(2,1)} custom-call(bf16[2,4,80,192]{3,2,1,0:T(8,128)(2,1)S(1)} %get-tuple-element.14.x_ref, bf16[2,192,768]{2,1,0:T(8,128)(2,1)S(1)} %get-tuple-element.15.w1s, f32[1,384]{1,0:T(1,128)S(1)} %get-tuple-element.16.b1_ref, f32[1,384]{1,0:T(1,128)S(1)} %get-tuple-element.17.g1_ref, ...), custom_call_target="tpu_custom_call" | custom-call | tf_op jit(solution)/shard_map/pallas_call | solution.py:497

commit v5 on v4

--- a/solution.py
+++ b/solution.py
@@ -190,7 +190,7 @@
         pltpu.make_async_copy(b2_hbm, b2buf, weight_sem.at[7]),
         pltpu.make_async_copy(g2_hbm, g2buf, weight_sem.at[8]),
     ]
-    for copy in loads + planes + weights:
+    for copy in planes[:1] + loads + planes[1:]:
         copy.start()
 
     barrier = pltpu.get_barrier_semaphore()
@@ -250,6 +250,9 @@
 
     for f in range(frames):
         planes[f].wait()
+        if f == 0:
+            for copy in weights:
+                copy.start()
         block = xbuf[f]
         full = jnp.dot(stack, block, preferred_element_type=F32)
         values = block.astype(F32)

time: 25.1 us -> 24.6 us (0.980)
  Pallas kernels: 25 us -> 24.4 us
    pallas_call x1, Pallas kernels: 20.8 us -> 20.2 us  [local(): pl.pallas_call(functools.partial(exchange_kernel, num_dev), out_shape=[ja...]
where the time goes in v5:
time: 24.6 us; the launch traced here: 24.4 us
  Pallas kernels  24.4 us (99%)
    pallas_call x1, Pallas kernels, local(): pl.pallas_call(functools.partial(exchange_kernel, num_dev), out_shape=[ja...  20.2 us
    pallas_call x1, Pallas kernels, local(): pl.pallas_call(functools.partial(conv_kernel, num_dev, c2), out_shape=jax...  4.17 us

profile of v5, /device:TPU:1, one launch (start us, length us, event | category | flops | bytes accessed | tf_op | source)
XLA Modules:
  0.0 24.4 jit_solution(8638126737954184608)
XLA Ops:
  0.0 20.2 %shard_map.127 = (bf16[2,4,80,192]{3,2,1,0:T(8,128)(2,1)S(1)}, bf16[2,192,768]{2,1,0:T(8,128)(2,1)S(1)}, bf16[2,768,768]{2,1,0:T(8,128)(2,1)S(1)}, bf16[2,3,768,...) custom-call(bf16[2,320,1280]{2,1,0:T(8,128)(2,1)} %x_hbm.1, ...), custom_call_target="tpu_custom_call" | custom-call | tf_op jit(solution)/shard_map/pallas_call | solution.py:445
  20.2 4.2 %shard_map.128 = bf16[8,96,320]{2,1,0:T(8,128)(2,1)} custom-call(bf16[2,4,80,192]{3,2,1,0:T(8,128)(2,1)S(1)} %get-tuple-element.14.x_ref, bf16[2,192,768]{2,1,0:T(8,128)(2,1)S(1)} %get-tuple-element.15.w1s, f32[1,384]{1,0:T(1,128)S(1)} %get-tuple-element.16.b1_ref, f32[1,384]{1,0:T(1,128)S(1)} %get-tuple-element.17.g1_ref, ...), custom_call_target="tpu_custom_call" | custom-call | tf_op jit(solution)/shard_map/pallas_call | solution.py:500
